TPU v7x, 32 devices: a whole 2x2x4 slice. The times are simulated.
32 devices in a mesh: ctx: 8 (over z, y), head: 2 (over x), section: 2 (over core).
Axes of the slice: x: 2, y: 2, z: 4, core: 2. Of those that a mesh axis runs over, the one named last changes fastest.
Arguments:
- delta_query: bfloat16 [2, 1024, 2048], P('section', 'ctx', 'head'), may hold values from -6 to 6
- delta_key: bfloat16 [2, 1024, 2048], P('section', 'ctx', 'head'), may hold values from -6 to 6
- delta_value: bfloat16 [2, 1024, 2048], P('section', 'ctx', 'head'), may hold values from -6 to 6
- beta_logit: float32 [2, 1024, 16], P('section', 'ctx', 'head'), may hold values from -6 to 6
- decay_input: float32 [2, 1024, 16], P('section', 'ctx', 'head'), may hold values from -4 to 9216
- decay_log: float32 [16], P('head'), may hold values from -14 to -2
- norm_gain: float32 [128], replicated, may hold values from 0.25 to 1.75
- output_gate: bfloat16 [2, 1024, 2048], P('section', 'ctx', 'head'), may hold values from -6 to 6
- delta_cotangent: bfloat16 [2, 1024, 2048], P('section', 'ctx', 'head'), may hold values from -12 to 12
- attn_query: bfloat16 [2, 1024, 4096], P('section', 'ctx', 'head'), may hold values from -5 to 5
- attn_key: bfloat16 [2, 1024, 512], P('section', 'ctx', 'head'), may hold values from -5 to 5
- attn_value: bfloat16 [2, 1024, 512], P('section', 'ctx', 'head'), may hold values from -6 to 6
- attn_gate: bfloat16 [2, 1024, 4096], P('section', 'ctx', 'head'), may hold values from -6 to 6
- attn_cotangent: bfloat16 [2, 1024, 4096], P('section', 'ctx', 'head'), may hold values from -6 to 6
Outputs:
- delta_output: bfloat16 [2, 1024, 2048], P('section', 'ctx', 'head')
- grad_delta_query: bfloat16 [2, 1024, 2048], P('section', 'ctx', 'head')
- grad_delta_key: bfloat16 [2, 1024, 2048], P('section', 'ctx', 'head')
- grad_delta_value: bfloat16 [2, 1024, 2048], P('section', 'ctx', 'head')
- grad_beta_logit: float32 [2, 1024, 16], P('section', 'ctx', 'head')
- grad_decay_input: float32 [2, 1024, 16], P('section', 'ctx', 'head')
- grad_decay_log: float32 [16], P('head')
- grad_norm_gain: float32 [128], replicated
- grad_output_gate: bfloat16 [2, 1024, 2048], P('section', 'ctx', 'head')
- attn_output: bfloat16 [2, 1024, 4096], P('section', 'ctx', 'head')
- grad_attn_query: bfloat16 [2, 1024, 4096], P('section', 'ctx', 'head')
- grad_attn_key: bfloat16 [2, 1024, 512], P('section', 'ctx', 'head')
- grad_attn_value: bfloat16 [2, 1024, 512], P('section', 'ctx', 'head')
- grad_attn_gate: bfloat16 [2, 1024, 4096], P('section', 'ctx', 'head')
All inputs are finite; a program needn't handle non-finite values.
Results may differ from a plain program's by a relative error of at most 0.02.
Values may be sent and summed in bfloat16 or wider, within the bound.
No kernel may reach another device: no remote copies, remote signals or barrier semaphores. Data moves between devices by JAX's collectives and lax.ppermute only.
A program may use at most 256 MiB of HBM per device.

v0:
```python
import functools
import jax
import jax.numpy as jnp
from jax import lax
from jax.experimental import pallas as pl
from jax.experimental.pallas import tpu as pltpu
from jax.sharding import PartitionSpec as P

AD = 256
F32 = jnp.float32
BF = jnp.bfloat16
HIGHEST = lax.Precision.HIGHEST
DECAY_FLOOR = -110.0
NEG_FILL = -1e30
KQ = F32
INV = F32
SCO = F32
UPD = F32
KRE = F32
DY = F32
DX = F32
GDX = F32
MK = F32
OUTER = F32
VMEM_LIMIT = 20 << 20


def plain_dot(a, b, ca, cb, precision=None):
    return lax.dot_general(
        a, b, (((ca,), (cb,)), ((), ())), preferred_element_type=F32, precision=precision
    )


def halves(x):
    high = x.astype(BF)
    return high, (x - high.astype(F32)).astype(BF)


def dot(a, b, ca=1, cb=0, precision=None):
    wide_a, wide_b = a.dtype == F32, b.dtype == F32
    if precision is not None or not (wide_a or wide_b):
        return plain_dot(a, b, ca, cb, precision)
    ah, al = halves(a) if wide_a else (a, a)
    bh, bl = halves(b) if wide_b else (b, b)
    if not wide_a:
        return plain_dot(jnp.concatenate([a, a], ca), jnp.concatenate([bh, bl], cb), ca, cb)
    first = plain_dot(jnp.concatenate([ah, al], ca), jnp.concatenate([bh, bh], cb), ca, cb)
    return first + plain_dot(ah, bl, ca, cb) if wide_b else first


def mm3(a, b):
    return dot(a, b)


def interleave(steps):
    steps = list(steps)
    while steps:
        steps = [step for step in steps if next(step, step) is not step]


def ids(rows, cols):
    return (
        lax.broadcasted_iota(jnp.int32, (rows, cols), 0),
        lax.broadcasted_iota(jnp.int32, (rows, cols), 1),
    )


def head_cols(base, slot, width):
    return pl.ds(pl.multiple_of((base ^ slot) * width, width), width)


def unit_of(x):
    inv = lax.rsqrt(jnp.sum(x * x, axis=-1, keepdims=True) + 1e-06)
    return x * inv, inv


def slot_matrix(base, heads, lanes):
    row, col = ids(lanes, lanes)
    return jnp.where((row == (col ^ base)) & (col < heads), 1.0, 0.0).astype(F32)


def softplus(x):
    return jnp.maximum(x, 0.0) + jnp.log(1.0 + jnp.exp(-jnp.abs(x)))


def sigmoid(x):
    return 1.0 / (1.0 + jnp.exp(-x))


def rate_of(log_ref, heads):
    row, col = ids(heads, heads)
    return jnp.sum(jnp.where(row == col, -jnp.exp(log_ref[...]), 0.0), axis=1, keepdims=True)


def fetch(sources, targets, sems):
    copies = [
        pltpu.make_async_copy(source, target, sems.at[i])
        for i, (source, target) in enumerate(zip(sources, targets))
    ]
    for copy in copies:
        copy.start()
    return copies


def fetch_all(sources, targets, sems):
    for copy in fetch(sources, targets, sems):
        copy.wait()


def prepare_kernel(heads, base_ref, *refs):
    sources, refs = refs[:6], refs[6:]
    inputs, sems = refs[15:21], refs[21]
    copies = fetch(sources, inputs, sems)
    q_ref, k_ref, v_ref, beta_ref, decay_ref, log_ref = inputs
    refs = refs[:15]
    half = heads // 2
    base = (base_ref[0] & 1) * (heads // 2)
    g_ref, b_ref, pad = refs[12:]
    perm = slot_matrix(base, heads, pad.shape[0])
    pad[...] = jnp.zeros_like(pad)
    for copy in copies[3:]:
        copy.wait()
    pad[:heads, :] = sigmoid(beta_ref[...])
    b_ref[...] = dot(pad[...], perm, 0, 0, precision=HIGHEST)
    pad[:heads, :] = jnp.maximum(rate_of(log_ref, heads) * softplus(decay_ref[...]), DECAY_FLOOR)
    decays = dot(pad[...], perm, 0, 0, precision=HIGHEST)
    rows = g_ref.shape[0]
    size = refs[1].shape[2]
    row, col = ids(rows, rows)
    within = row >= col
    strict = row > col
    g_all = dot(jnp.where(within, 1.0, 0.0).astype(F32), decays, precision=HIGHEST)
    g_ref[...] = g_all
    betas = b_ref[...]
    g_rows = g_all.T
    identity = jnp.where(row == col, 1.0, 0.0).astype(F32)
    small = 16
    copies[0].wait()
    copies[1].wait()
    units, lowers, inverses = [], [], []

    def begin(s):
        _, kb_ref, qb_ref, _, p_ref, n_ref = refs[6 * (s // half) : 6 * (s // half) + 6]
        i = s % half
        cols = head_cols(base, s, size)
        unit_q = unit_of(q_ref[:, cols].astype(F32))[0] * (size**-0.5)
        unit_k = unit_of(k_ref[:, cols].astype(F32))[0]
        qb = unit_q.astype(KQ)
        kb = unit_k.astype(KQ)
        qb_ref[i] = qb
        kb_ref[i] = kb
        yield
        fade = jnp.exp(jnp.where(within, g_all[:, s : s + 1] - g_rows[s : s + 1, :], 0.0))
        both = dot(jnp.concatenate([kb, qb], 0), kb, 1, 1)
        yield
        plain = jnp.where(strict, fade * both[:rows], 0.0)
        n_ref[i] = plain.astype(n_ref.dtype)
        p_ref[i] = jnp.where(within, fade * both[rows:], 0.0).astype(SCO)
        lower = betas[:, s : s + 1] * plain
        lowers.append(lower)
        diag = jnp.where((row // small) == (col // small), lower, 0.0)
        units.append(diag)
        inverses.append(identity - diag)

    interleave(begin(s) for s in range(heads))
    span = 2
    while span < small:
        units = [mm3(x, x) for x in units]
        inverses = [x + mm3(x, y) for x, y in zip(inverses, units)]
        span *= 2
    span = small
    while span < rows:
        pick = ((row // (2 * span)) == (col // (2 * span))) & ((row // span) != (col // span))
        inner = [mm3(jnp.where(pick, x, 0.0), y) for x, y in zip(lowers, inverses)]
        inverses = [x - mm3(x, y) for x, y in zip(inverses, inner)]
        span *= 2
    row_k, col_k = ids(size, size)
    copies[2].wait()

    def finish(s):
        maps_ref, kb_ref, _, m_ref, _, _ = refs[6 * (s // half) : 6 * (s // half) + 6]
        i = s % half
        cols = head_cols(base, s, size)
        gc = g_all[:, s : s + 1]
        beta = betas[:, s : s + 1]
        end = g_rows[s : s + 1, rows - 1 : rows]
        unit_k = kb_ref[i].astype(F32)
        mb = inverses[s].astype(INV)
        m_ref[i] = mb
        right = jnp.concatenate(
            [(beta * jnp.exp(gc) * unit_k).astype(OUTER), (beta * v_ref[:, cols].astype(F32)).astype(OUTER)], 1
        )
        parts = dot(mb, right)
        yield
        tail = (jnp.exp(end - gc) * unit_k).astype(OUTER)
        both = dot(tail, parts.astype(OUTER), 0, 0)
        yield
        carry = jnp.where(row_k == col_k, jnp.exp(end), 0.0) - both[:, :size]
        maps_ref[i] = jnp.concatenate([carry, both[:, size:]], 1).astype(BF)

    interleave(finish(s) for s in range(heads))


def precise(carry, state, ca=1):
    high, low = halves(state)
    return dot(carry, high, ca, 0) + dot(carry, low, ca, 0)


def bit_of(here_ref, level):
    return (here_ref[0] >> level) & 1


def up_kernel(level, here_ref, own_ref, recv_ref, pair_ref, total_ref):
    bit = bit_of(here_ref, level)
    size = own_ref.shape[1]
    pair_ref[bit] = own_ref[...]
    pair_ref[1 - bit] = recv_ref[...]
    full = total_ref.shape[2] > size
    for i in range(own_ref.shape[0]):
        low, high = pair_ref[0, i], pair_ref[1, i]
        moved = dot(high[:, :size], low if full else low[:, size:])
        if full:
            total_ref[i, :, :size] = moved[:, :size].astype(BF)
            moved = moved[:, size:]
        total_ref[i, :, total_ref.shape[2] - size :] = (
            moved + high[:, size:].astype(F32)
        ).astype(BF)


def down_kernel(levels, here_ref, top_ref, *refs):
    pairs, (own_ref, send_ref) = refs[:-2], refs[-2:]
    size = top_ref.shape[1]

    def one(i):
        state = jnp.where(bit_of(here_ref, levels - 1) == 1, top_ref[i].astype(F32), 0.0)
        for level in range(levels - 2, -1, -1):
            low = pairs[level][0, i]
            later = precise(low[:, :size], state) + low[:, size:].astype(F32)
            yield
            first = bit_of(here_ref, level) == 0
            if level:
                state = jnp.where(first, state, later)
        own_ref[i] = jnp.where(first, state, later).astype(BF)
        send_ref[i] = jnp.where(first, later, state).astype(BF)

    interleave(one(i) for i in range(top_ref.shape[0]))


def up_back_kernel(
    level, count, here_ref, pair_ref, own_ref, recv_ref, mine_ref, locals_ref, total_ref
):
    bit = bit_of(here_ref, level)
    size = pair_ref.shape[2]
    locals_ref[bit] = own_ref[...]
    locals_ref[1 - bit] = recv_ref[...]
    for i in range(count):
        part = pl.ds(i * size, size)
        moved = dot(pair_ref[0, i][:, :size], locals_ref[1, part, :], 0, 0)
        total_ref[part, :] = (moved + locals_ref[0, part, :].astype(F32)).astype(BF)
    add_gain(total_ref, count * size, mine_ref, recv_ref)


def gain_rows(value):
    high, low = halves(value)
    row = lax.broadcasted_iota(jnp.int32, (16, value.shape[1]), 0)
    high, low = high.astype(F32), low.astype(F32)
    return jnp.where(row == 0, high, jnp.where(row == 1, low, 0.0)).astype(BF)


def gain_of(ref, start):
    return jnp.sum(ref[start : start + 16, :].astype(F32), axis=0, keepdims=True)


def add_gain(out_ref, start, own_ref, recv_ref):
    out_ref[start : start + 16, :] = gain_rows(gain_of(own_ref, start) + gain_of(recv_ref, start))


def down_back_kernel(levels, count, here_ref, mine_ref, top_ref, *refs):
    pairs, locals_ = refs[: levels - 1], refs[levels - 1 : 2 * levels - 2]
    own_ref, send_ref, gain_ref = refs[2 * levels - 2 :]
    size = own_ref.shape[1]

    def one(i):
        part = pl.ds(i * size, size)
        state = jnp.where(bit_of(here_ref, levels - 1) == 0, top_ref[part, :].astype(F32), 0.0)
        for level in range(levels - 2, -1, -1):
            earlier = precise(pairs[level][1, i][:, :size], state, 0) + locals_[level][
                1, part, :
            ].astype(F32)
            yield
            first = bit_of(here_ref, level) == 0
            if level:
                state = jnp.where(first, earlier, state)
        own_ref[i] = jnp.where(first, earlier, state).astype(BF)
        send_ref[i] = jnp.where(first, state, earlier).astype(BF)

    interleave(one(i) for i in range(count))
    gain_ref[...] = gain_of(mine_ref, count * size) + gain_of(top_ref, count * size)


def fixed_cols(i, size):
    return slice(i * size, (i + 1) * size)


def output_kernel(
    heads, first, base_ref, state_ref, v_ref, gate_ref, cot_ref, gain_ref, kb_ref, qb_ref, m_ref,
    p_ref, g_ref, b_ref, *refs,
):
    local_ref, u_ref, kre_ref, dy_ref, dx_ref, dg_ref, total_ref, out_ref, dgate_ref = refs[-9:]
    half = heads // 2
    base = (base_ref[0] & 1) * (heads // 2)
    rows = u_ref.shape[1]
    size = kb_ref.shape[2]
    gain = gain_ref[...]
    totals = []
    dg_ref[...] = jnp.zeros_like(dg_ref)

    def one(i):
        s = first + i
        cols, fixed = head_cols(base, s, size), fixed_cols(i, size)
        kb, qb = kb_ref[i], qb_ref[i]
        eg = jnp.exp(g_ref[:, s : s + 1])
        beta = b_ref[:, s : s + 1]
        both = dot(jnp.concatenate([kb, qb], 0), state_ref[i])
        yield
        kre = (eg * both[:rows]).astype(KRE)
        qre = eg * both[rows:]
        kre_ref[i] = kre
        rest = beta * (v_ref[:, cols].astype(F32) - kre.astype(F32))
        mb, pb = m_ref[i], p_ref[i]
        update = dot(mb, rest.astype(UPD)).astype(UPD)
        yield
        u_ref[i] = update
        mix = qre + dot(pb, update)
        yield
        inv = lax.rsqrt(jnp.mean(mix * mix, axis=-1, keepdims=True) + 1e-06)
        norm = mix * inv
        gate = gate_ref[:, cols].astype(F32)
        opening = sigmoid(gate)
        silu = gate * opening
        cot = cot_ref[:, cols].astype(F32)
        normed = norm * gain
        out_ref[:, fixed] = (normed * silu).astype(BF)
        dgate_ref[:, fixed] = (
            cot * normed * (opening * (1.0 + gate * (1.0 - opening)))
        ).astype(BF)
        weighted = cot * silu
        totals.append(jnp.sum(weighted * norm, axis=0, keepdims=True))
        dnorm = weighted * gain
        dmix = inv * (dnorm - norm * jnp.mean(dnorm * norm, axis=-1, keepdims=True))
        dy = dmix.astype(DY)
        dy_ref[i] = dy
        dg_ref[:, s : s + 1] = jnp.sum(qre * dmix, axis=-1, keepdims=True)
        yield
        moved = dot(pb, dy, 0, 0).astype(DX)
        yield
        dx = dot(mb, moved, 0, 0)
        yield
        dx_ref[i] = dx
        left = jnp.concatenate([qb, kb], 0)
        right = jnp.concatenate(
            [(eg * dmix).astype(OUTER), (-(eg * beta) * dx).astype(OUTER)], 0
        )
        local_ref[pl.ds(i * size, size), :] = dot(left, right, 0, 0).astype(BF)

    interleave(one(i) for i in range(half))
    total = sum(totals[1:], totals[0])
    if len(refs) > 9:
        total = total + refs[0][...]
    total_ref[...] = total
    local_ref[half * size : half * size + 16, :] = gain_rows(total)


def query_kernel(heads, base_ref, q_ref, g_ref, *refs):
    half = heads // 2
    dgc_ref, dgr_ref, dq_ref = refs[-3:]
    base = (base_ref[0] & 1) * (heads // 2)
    rows = dq_ref.shape[0]
    size = refs[0].shape[2]
    row, col = ids(rows, rows)
    within = row >= col
    g_all = g_ref[...]
    g_rows = g_all.T
    dgc_ref[...] = refs[7][...] + refs[15][...]
    dgr_ref[...] = jnp.zeros_like(dgr_ref)

    def one(s):
        i, side = s % half, s // half
        state_ref, kb_ref, qb_ref, m_ref, p_ref, u_ref, dy_ref, _ = refs[8 * side : 8 * side + 8]
        dkp_ref, mk_ref = refs[16 + 2 * side : 18 + 2 * side]
        cols = head_cols(base, s, size)
        kb, qb, dy, pb = kb_ref[i], qb_ref[i], dy_ref[i], p_ref[i]
        gc = g_all[:, s : s + 1]
        end = g_rows[s : s + 1, rows - 1 : rows]
        fade = jnp.exp(jnp.where(within, gc - g_rows[s : s + 1, :], 0.0))
        dp = dot(dy, u_ref[i], 1, 1)
        yield
        dpf = jnp.where(within, dp * fade, 0.0).astype(BF)
        moved = dp * pb.astype(F32)
        dgc_ref[:, s : s + 1] += jnp.sum(moved, axis=1, keepdims=True)
        dgr_ref[s : s + 1, :] = -jnp.sum(moved, axis=0, keepdims=True)
        left = jnp.concatenate([(jnp.exp(gc) * dy.astype(F32)).astype(BF), dpf], 1)
        right = jnp.concatenate([state_ref[i].T, kb.astype(BF)], 0)
        dunit = dot(left, right)
        yield
        unit, inv = unit_of(q_ref[:, cols].astype(F32))
        dq_ref[:, cols] = (
            (inv * size**-0.5) * (dunit - unit * jnp.sum(unit * dunit, axis=-1, keepdims=True))
        ).astype(BF)
        dkp_ref[i] = dot(dpf, qb.astype(BF), 0, 0)
        tail = (jnp.exp(end - gc) * kb.astype(F32)).astype(MK)
        mk_ref[i] = dot(m_ref[i], tail, 0, 0).astype(MK)
        yield

    interleave(one(s) for s in range(heads))


def decay_kernel(
    heads, first, final, base_ref, state_ref, grad_ref, k_ref, v_ref, n_ref, g_ref, b_ref, u_ref, kre_ref,
    dx_ref, mk_ref, dgc_in, dgr_in, *refs,
):
    if not final:
        dmat_ref, dtail_ref, gdv_ref, dgc, dgr, dbc, dv_ref = refs
        dgc[...] = dgc_in[...]
        dgr[...] = dgr_in[...]
        dbc[...] = jnp.zeros_like(dbc)
    else:
        (
            decay_ref, log_ref, dbc_far, gain_ref, _, dmat_ref, dtail_ref, gdv_ref, dbeta_ref,
            ddecay_ref, small_ref, dv_ref, dgc, dgr, dbc, pad,
        ) = refs
        dgc[...] = dgc_in[...]
        dgr[...] = dgr_in[...]
        dbc[...] = dbc_far[...]
    base = (base_ref[0] & 1) * (heads // 2)
    rows = dv_ref.shape[0]
    size = mk_ref.shape[2]
    lanes = g_ref.shape[1]
    row, col = ids(rows, rows)
    within = row >= col
    strict = row > col
    last = lax.broadcasted_iota(jnp.int32, (rows, 1), 0) == rows - 1
    g_all = g_ref[...]
    g_rows = g_all.T

    def one(i):
        s = first + i
        cols = head_cols(base, s, size)
        update = u_ref[i]
        gc = g_all[:, s : s + 1]
        beta = b_ref[:, s : s + 1]
        end = g_rows[s : s + 1, rows - 1 : rows]
        state, grad = state_ref[i], grad_ref[i]
        fade = jnp.exp(jnp.where(within, gc - g_rows[s : s + 1, :], 0.0))
        dx = dx_ref[i] + dot(mk_ref[i], grad)
        yield
        kre = kre_ref[i].astype(F32)
        dv = beta * dx
        dv_ref[:, fixed_cols(i, size)] = dv.astype(BF)
        gdv_ref[i] = (-jnp.exp(gc) * dv).astype(BF)
        da = jnp.where(strict, -dot(dx.astype(GDX), update, 1, 1), 0.0)
        yield
        by_beta = da * n_ref[i].astype(F32)
        moved = beta * by_beta
        dbc[:, s : s + 1] = jnp.sum(
            by_beta + dx * (v_ref[:, cols].astype(F32) - kre), axis=1, keepdims=True
        )
        dmat_ref[i] = (da * (beta * fade)).astype(BF)
        dtail = jnp.exp(end - gc) * dot(update, grad, 1, 1)
        yield
        dtail_ref[i] = dtail
        unit = unit_of(k_ref[:, cols].astype(F32))[0]
        ends = dtail * unit
        dend = jnp.sum(
            jnp.sum(ends, axis=0, keepdims=True)
            + jnp.exp(end)
            * jnp.sum(state.astype(F32) * grad.astype(F32), axis=0, keepdims=True),
            axis=1,
            keepdims=True,
        )
        dgc[:, s : s + 1] = (
            dgc[:, s : s + 1]
            + jnp.sum(moved - ends - kre * dv, axis=1, keepdims=True)
            + jnp.where(last, dend, 0.0)
        )
        dgr[s : s + 1, :] = dgr[s : s + 1, :] - jnp.sum(moved, axis=0, keepdims=True)

    interleave(one(i) for i in range(heads // 2))
    if not final:
        return
    perm = slot_matrix(base, heads, lanes)
    ahead = jnp.where(row <= col, 1.0, 0.0).astype(F32)
    ddecay = dot(
        perm, dot(ahead, dgc[...] + dgr[...].T, precision=HIGHEST), 1, 1, precision=HIGHEST
    )[:heads]
    betas = b_ref[...]
    dbeta = dot(perm, dbc[...] * betas * (1.0 - betas), 1, 1, precision=HIGHEST)
    dbeta_ref[...] = dbeta[:heads]
    rate = rate_of(log_ref, heads)
    inputs = decay_ref[...]
    ddecay_ref[...] = ddecay * rate * sigmoid(inputs)
    pad[...] = jnp.zeros_like(pad)
    pad[:heads, :] = ddecay * rate * softplus(inputs)
    small_ref[0:1, :] = jnp.sum(pad[...].T, axis=0, keepdims=True)
    small_ref[1:2, :] = gain_ref[...]


def key_kernel(heads, base_ref, k_ref, *refs):
    half = heads // 2
    dk_ref = refs[-1]
    base = (base_ref[0] & 1) * (heads // 2)
    size = refs[0].shape[2]

    def one(s):
        i, side = s % half, s // half
        state_ref, kb_ref, dkp_ref, gdv_ref, dmat_ref, dtail_ref = refs[6 * side : 6 * side + 6]
        cols = head_cols(base, s, size)
        dmat = dmat_ref[i].astype(F32)
        left = jnp.concatenate([(dmat + dmat.T).astype(BF), gdv_ref[i]], 1)
        right = jnp.concatenate([kb_ref[i].astype(BF), state_ref[i].T], 0)
        yield
        dunit = dkp_ref[i] + dot(left, right) + dtail_ref[i]
        yield
        unit, inv = unit_of(k_ref[:, cols].astype(F32))
        dk_ref[:, cols] = (
            inv * (dunit - unit * jnp.sum(unit * dunit, axis=-1, keepdims=True))
        ).astype(BF)

    interleave(one(s) for s in range(heads))


def pair_kernel(_, first_ref, second_ref, out_ref, sems):
    cut = first_ref.shape[1]
    fetch_all((first_ref, second_ref), (out_ref.at[0, :, :cut], out_ref.at[0, :, cut:]), sems)


def join_kernel(_, first_ref, second_ref, out_ref):
    cut = first_ref.shape[0]
    out_ref[:cut] = first_ref[...]
    out_ref[cut:] = second_ref[...]


def attention_kernel(offsets, start, end, here_ref, q_ref, gate_ref, cot_ref, near_ref, far_ref, *refs):
    raised_ref, weights_ref, score_ref = refs[-3:]
    if start:
        ins, outs = (), refs[:-3]
    else:
        ins, outs = refs[:3], refs[6:-3]
    out_ref, dq_ref, dgate_ref = outs[:3]
    count = len(offsets)
    half = count // 2
    here = here_ref[0]
    rows = q_ref.shape[0]
    size = near_ref.shape[2] // 2
    group = q_ref.shape[1] // size
    wide = group * rows
    scaling = size**-0.5

    def keys_of(k):
        return (near_ref if k < half else far_ref)[k % half][:, :size]

    def values_of(k):
        return (near_ref if k < half else far_ref)[k % half][:, size:]

    if start:
        keys_t, values_t = outs[3:5]
        for k in range(count):
            part = pl.ds(k * rows, rows)
            keys_t[:, part] = keys_of(k).T
            values_t[:, part] = values_of(k).T
    else:
        keys_t, values_t, total_in = ins

    def stack(ref):
        return jnp.concatenate([ref[:, i * size : (i + 1) * size] for i in range(group)], 0)

    def spread(ref, value):
        for i in range(group):
            ref[:, i * size : (i + 1) * size] = value[i * rows : (i + 1) * rows].astype(ref.dtype)

    queries = (stack(q_ref).astype(F32) * scaling).astype(BF)
    key_at, query_at = ids(rows, wide)
    own = key_at <= (query_at % rows)
    top = jnp.full((1, wide), NEG_FILL, F32)
    biases = [jnp.where((here ^ x) < here, 0.0, NEG_FILL) if x else 0.0 for x in offsets]
    for k in range(count):
        scores = dot(keys_of(k), queries, 1, 1)
        if offsets[k] == 0:
            scores = jnp.where(own, scores, NEG_FILL)
        raised_ref[pl.ds(k * rows, rows), :] = scores
        top = jnp.maximum(top, jnp.max(scores, axis=0, keepdims=True) + biases[k])
    total = jnp.zeros((1, wide), F32)
    for k in range(count):
        part = pl.ds(k * rows, rows)
        raised = jnp.exp(raised_ref[part, :] - (top - biases[k]))
        raised_ref[part, :] = raised
        total = total + jnp.sum(raised, axis=0, keepdims=True)
    scale = 1.0 / total
    for k in range(count):
        part = pl.ds(k * rows, rows)
        weights_ref[part, :] = (raised_ref[part, :] * scale).astype(BF)
    attended_t = dot(values_t[...], weights_ref[...])
    attended = attended_t.T
    gate = stack(gate_ref).astype(F32)
    cot = stack(cot_ref).astype(F32)
    opening = sigmoid(gate)
    spread(out_ref, attended * opening)
    up = (cot * opening).astype(BF)
    spread(dgate_ref, cot * attended * opening * (1.0 - opening))
    up_t = up.T
    centering = jnp.sum(up_t.astype(F32) * attended_t, axis=0, keepdims=True) * scale
    for k in range(count):
        part = pl.ds(k * rows, rows)
        weight_grad = dot(values_of(k), up_t)
        score_ref[part, :] = (raised_ref[part, :] * (weight_grad * scale - centering)).astype(BF)
    dq_t = dot(keys_t[...], score_ref[...]) * scaling
    spread(dq_ref, dq_t.T)
    dk = dot(score_ref[...], queries)
    dv = dot(weights_ref[...], up)
    for k in range(count):
        part = slice(k * rows, (k + 1) * rows)
        if end:
            target, at = (outs[3] if k < half else outs[4]), k % half
        else:
            target, at = outs[-1], k
        dk_part, dv_part = dk[part], dv[part]
        if not start:
            dk_part = dk_part + total_in[k, :, :size]
            dv_part = dv_part + total_in[k, :, size:]
        target[at, :, :size] = dk_part.astype(target.dtype)
        target[at, :, size:] = dv_part.astype(target.dtype)


def call(kernel, outs, scratch, base, *args, blocked=(), prior=None, side=0, far=False):
    vmem = pl.BlockSpec(memory_space=pltpu.VMEM)
    hbm = pl.BlockSpec(memory_space=pl.ANY)
    if far:
        args = tuple(pltpu.with_memory_space_constraint(x, pltpu.HBM) for x in args)
    args = tuple(args) + tuple(prior or ())
    count = len(args) + 1 - len(prior or ())
    return pl.pallas_call(
        kernel,
        out_shape=tuple(jax.ShapeDtypeStruct(shape, dtype) for shape, dtype in tuple(outs) + tuple(blocked)),
        grid_spec=pltpu.PrefetchScalarGridSpec(
            num_scalar_prefetch=1,
            grid=(1,),
            in_specs=[pl.BlockSpec(memory_space=pltpu.HBM) if far else vmem] * (count - 1) + [hbm] * len(prior or ()),
            out_specs=tuple(vmem for _ in outs)
            + tuple(
                pl.BlockSpec((shape[0], shape[1] // 2), lambda i, where: (0, (where[0] & 1) ^ side))
                for shape, _ in blocked
            ),
            scratch_shapes=scratch,
        ),
        input_output_aliases={count + i: len(outs) + i for i in range(len(prior or ()))},
        compiler_params=pltpu.CompilerParams(vmem_limit_bytes=VMEM_LIMIT),
    )(base, *args)


def swap(value, axis, offset):
    count = lax.axis_size(axis)
    return lax.ppermute(value, axis, [(i, i ^ offset) for i in range(count)])


def axis_sum(value, axis):
    offset = 1
    while offset < lax.axis_size(axis):
        value = value + swap(value, axis, offset)
        offset *= 2
    return value


def per_device(
    delta_query,
    delta_key,
    delta_value,
    beta_logit,
    decay_input,
    decay_log,
    norm_gain,
    output_gate,
    delta_cotangent,
    attn_query,
    attn_key,
    attn_value,
    attn_gate,
    attn_cotangent,
):
    tokens = delta_query.shape[1]
    heads = decay_log.shape[0]
    size = norm_gain.shape[0]
    lanes = 128
    count = lax.axis_size("ctx")
    levels = count.bit_length() - 1
    here = lax.axis_index("ctx").astype(jnp.int32)
    half = heads // 2
    spot = here.reshape(1)

    rows_att, key_width = attn_key.shape[1], attn_key.shape[2]
    (near_kv,) = call(
        pair_kernel, [((1, rows_att, 2 * key_width), BF)], [pltpu.SemaphoreType.DMA((2,))],
        spot, attn_key[0], attn_value[0], far=True,
    )
    offsets = [0]
    jump = count // 2
    while jump > 1:
        moved = swap(near_kv, "ctx", jump)
        (near_kv,) = call(
            join_kernel,
            [((2 * near_kv.shape[0],) + near_kv.shape[1:], BF)], [], spot, near_kv, moved,
        )
        offsets += [x ^ jump for x in offsets]
        jump //= 2
    far_kv = swap(near_kv, "ctx", 1)
    offsets += [x ^ 1 for x in offsets]

    q, k, v = delta_query[0], delta_key[0], delta_value[0]
    beta, decay, logs = beta_logit[0].T, decay_input[0].T, decay_log[None]
    column = ((tokens, lanes), F32)
    turned = ((lanes, tokens), F32)
    flat = ((tokens, heads * size), BF)
    small = ((heads, tokens), F32)
    maps = ((half, size, 2 * size), BF)
    states = ((half, size, size), BF)
    cube = ((half, tokens, size), BF)
    cube_wide = ((half, tokens, size), F32)
    square = ((half, tokens, tokens), BF)
    packed = ((half * size + 16, size), BF)
    column_scratch = pltpu.VMEM(*column)

    kept = [maps, (cube[0], KQ), (cube[0], KQ), (square[0], INV), (square[0], SCO), (square[0], SCO)]
    results = call(
        functools.partial(prepare_kernel, heads), kept + kept + [column, column],
        [pltpu.VMEM(*turned)]
        + [pltpu.VMEM(x.shape, x.dtype) for x in (q, k, v, beta, decay, logs)]
        + [pltpu.SemaphoreType.DMA((6,))],
        spot, q, k, v, beta, decay, logs, far=True,
    )
    keep, *near = results[:6]
    send, *far = results[6:12]
    g, b = results[12:]
    pairs = []
    for level in range(levels - 1):
        moved = swap(send, "ctx", 1 << level)
        pair, total = call(
            functools.partial(up_kernel, level),
            [((2,) + maps[0], BF), maps if level < levels - 2 else states],
            [], spot, keep, moved,
        )
        pairs.append(pair)
        keep = send = total
    moved = swap(send, "ctx", 1 << (levels - 1))
    near_state, send = call(
        functools.partial(down_kernel, levels), [states, states], [], spot, moved, *pairs
    )
    far_state = swap(send, "ctx", 1)
    gain = norm_gain[None]
    gates = output_gate[0], delta_cotangent[0], gain
    kept = [packed, (cube[0], UPD), (cube[0], KRE), (cube[0], DY), cube_wide, column, ((1, size), F32)]
    keep, *near_out, dg_near, gain_near, out, dgate = call(
        functools.partial(output_kernel, heads, 0), kept, [],
        spot, near_state, v, *gates, near[0], near[1], near[2], near[3], g, b,
        blocked=[flat, flat],
    )
    send, *far_out, dg_far, _, out, dgate = call(
        functools.partial(output_kernel, heads, half), kept, [],
        spot, far_state, v, *gates, far[0], far[1], far[2], far[3], g, b, gain_near,
        blocked=[flat, flat], prior=[out, dgate], side=1,
    )
    locals_ = []
    for level in range(levels - 1):
        moved = swap(send, "ctx", 1 << level)
        both, total = call(
            functools.partial(up_back_kernel, level, half),
            [((2,) + packed[0], BF), packed],
            [], spot, pairs[level], keep, moved, send,
        )
        locals_.append(both)
        keep = send = total
    moved = swap(send, "ctx", 1 << (levels - 1))
    near_grad, send, gain_part = call(
        functools.partial(down_back_kernel, levels, half), [states, states, ((1, size), F32)], [],
        spot, keep, moved, *pairs, *locals_,
    )
    far_grad = swap(send, "ctx", 1)
    gain_part = axis_sum(gain_part, "head")
    dkp_near, mk_near, dkp_far, mk_far, dgc, dgr, dq = call(
        functools.partial(query_kernel, heads),
        [cube_wide, (cube[0], MK), cube_wide, (cube[0], MK), column, turned, flat], [], spot, q, g,
        near_state, near[0], near[1], near[2], near[3], near_out[0], near_out[2], dg_near,
        far_state, far[0], far[1], far[2], far[3], far_out[0], far_out[2], dg_far,
    )
    dmat_near, dtail_near, gdv_near, dgc, dgr, dbc, dv = call(
        functools.partial(decay_kernel, heads, 0, False),
        [square, cube_wide, cube, column, turned, column], [],
        spot, near_state, near_grad, k, v, near[4], g, b, near_out[0], near_out[1], near_out[3],
        mk_near, dgc, dgr,
        blocked=[flat],
    )
    dmat_far, dtail_far, gdv_far, dbeta, ddecay, sums, dv = call(
        functools.partial(decay_kernel, heads, half, True),
        [square, cube_wide, cube, small, small, ((2, lanes), F32)],
        [column_scratch, pltpu.VMEM(*turned), column_scratch, column_scratch],
        spot, far_state, far_grad, k, v, far[4], g, b, far_out[0], far_out[1], far_out[3],
        mk_far, dgc, dgr, decay, logs, dbc, gain_part,
        blocked=[flat], prior=[dv], side=1,
    )
    (dk,) = call(
        functools.partial(key_kernel, heads), [flat], [], spot, k,
        near_state, near[0], dkp_near, gdv_near, dmat_near, dtail_near,
        far_state, far[0], dkp_far, gdv_far, dmat_far, dtail_far,
    )
    sums = axis_sum(sums, "section")
    gain_grad = sums[1]
    log_grad = sums[:1]
    for level in range(levels):
        log_grad = log_grad + swap(log_grad, "ctx", 1 << level)

    groups = attn_query.shape[2] // AD
    group = 2 if groups % 2 == 0 else 1
    calls = groups // group
    length = count * rows_att
    vmem = pl.BlockSpec(memory_space=pltpu.VMEM)
    wide = jax.ShapeDtypeStruct((rows_att, groups * AD), BF)
    turned_kv = jax.ShapeDtypeStruct((AD, length), BF)
    terms = jax.ShapeDtypeStruct((count, rows_att, 2 * key_width), F32)
    extra, outs = [], []
    for j in range(calls):
        start, end = j == 0, j == calls - 1
        block = pl.BlockSpec((rows_att, group * AD), lambda i, where, j=j: (0, j))
        tail = [turned_kv, turned_kv] if start else []
        if end:
            tail = tail + [
                jax.ShapeDtypeStruct(near_kv.shape, F32), jax.ShapeDtypeStruct(near_kv.shape, BF)
            ]
        else:
            tail = tail + [terms]
        results = pl.pallas_call(
            functools.partial(attention_kernel, offsets, start, end),
            grid_spec=pltpu.PrefetchScalarGridSpec(
                num_scalar_prefetch=1,
                grid=(1,),
                in_specs=[block, block, block] + [vmem] * (2 + len(extra))
                + [pl.BlockSpec(memory_space=pl.ANY)] * len(outs),
                out_specs=[block, block, block] + [vmem] * len(tail),
                scratch_shapes=[
                    pltpu.VMEM((length, group * rows_att), dtype) for dtype in (F32, BF, BF)
                ],
            ),
            out_shape=[wide, wide, wide] + tail,
            input_output_aliases={6 + len(extra) + i: i for i in range(len(outs))},
            compiler_params=pltpu.CompilerParams(vmem_limit_bytes=VMEM_LIMIT),
        )(spot, attn_query[0], attn_gate[0], attn_cotangent[0], near_kv, far_kv, *extra, *outs)
        outs = results[:3]
        if start:
            keys_t, values_t = results[3:5]
        extra = [keys_t, values_t, results[-1]]
    attn_out, dquery, dgate_att = outs
    own, send = results[-2:]
    moved = swap(send, "ctx", 1)
    own = own + moved.astype(F32)
    jump = 2
    while jump < count:
        own, send = jnp.split(own, 2)
        send = send.astype(BF)
        moved = swap(send, "ctx", jump)
        own = own + moved.astype(F32)
        jump *= 2
    own = own[0].astype(BF)
    return (
        out[None],
        dq[None],
        dk[None],
        dv[None],
        dbeta.T[None],
        ddecay.T[None],
        log_grad[0, :heads],
        gain_grad,
        dgate[None],
        attn_out[None],
        dquery[None],
        own[:, :key_width][None],
        own[:, key_width:][None],
        dgate_att[None],
    )


def solution(mesh):
    split = P("section", "ctx", "head")
    in_specs = (split,) * 5 + (P("head"), P()) + (split,) * 7
    out_specs = (split,) * 6 + (P("head"), P()) + (split,) * 6

    return jax.shard_map(
        per_device, mesh=mesh, in_specs=in_specs, out_specs=out_specs, check_vma=False
    )
```

profile of v0, /device:TPU:0, one launch (start us, length us, event | category | flops | bytes accessed | tf_op | source)
XLA Modules:
  0.0 114.6 jit_solution(13049569670467783245)
XLA Ops:
  1.5 4.1 %collective-permute-start.13 = (bf16[1,128,512]{2,1,0:T(8,128)(2,1)S(1)}, bf16[1,128,512]{2,1,0:T(8,128)(2,1)S(1)}, u32[]{:S(2)}, u32[]{:S(2)}) collective-permute-start(bf16[1,128,512]{2,1,0:T(8,128)(2,1)S(1)} %shard_map.258.first_ref), channel_id=1, source_target_pairs={{0,16},{4,20},{8,24},{12,28},{16,0},{20,4},{24,8},{28,12},{1,17},{... | collective-permute-start | bytes 393224 | tf_op jit(solution)/shard_map/ppermute | solution.py:662
  5.7 6.3 %collective-permute-done.13.second_ref = bf16[1,128,512]{2,1,0:T(8,128)(2,1)S(1)} collective-permute-done((bf16[1,128,512]{2,1,0:T(8,128)(2,1)S(1)}, bf16[1,128,512]{2,1,0:T(8,128)(2,1)S(1)}, u32[]{:S(2)}, u32[]{:S(2)}) %collective-permute-start.13) | collective-permute-done | bytes 131104 | tf_op jit(solution)/shard_map/ppermute | solution.py:662
  12.8 6.7 %shard_map.245 = (bf16[4,128,256]{2,1,0:T(8,128)(2,1)S(1)}, f32[4,128,128]{2,1,0:T(8,128)S(1)}, f32[4,128,128]{2,1,0:T(8,128)S(1)}, f32[4,128,128]{2,1,0:T(8,128...) custom-call(s32[1]{0:T(128)} %bitcast.base_ref.here_ref._, ...), custom_call_target="tpu_custom_call" | custom-call | tf_op jit(solution)/shard_map/pallas_call | solution.py:641
  21.8 7.0 %collective-permute-done.recv_ref = bf16[4,128,256]{2,1,0:T(8,128)(2,1)S(1)} collective-permute-done((bf16[4,128,256]{2,1,0:T(8,128)(2,1)S(1)}, bf16[4,128,256]{2,1,0:T(8,128)(2,1)S(1)}, u32[]{:S(2)}, u32[]{:S(2)}) %collective-permute-start) | collective-permute-done | bytes 262176 | tf_op jit(solution)/shard_map/ppermute | solution.py:662
  30.5 5.1 %collective-permute-done.1.recv_ref = bf16[4,128,256]{2,1,0:T(8,128)(2,1)S(1)} collective-permute-done((bf16[4,128,256]{2,1,0:T(8,128)(2,1)S(1)}, bf16[4,128,256]{2,1,0:T(8,128)(2,1)S(1)}, u32[]{:S(2)}, u32[]{:S(2)}) %collective-permute-start.1) | collective-permute-done | bytes 262176 | tf_op jit(solution)/shard_map/ppermute | solution.py:662
  35.8 4.8 %collective-permute-start.2 = (bf16[4,128,128]{2,1,0:T(8,128)(2,1)S(1)}, bf16[4,128,128]{2,1,0:T(8,128)(2,1)S(1)}, u32[]{:S(2)}, u32[]{:S(2)}) collective-permute-start(bf16[4,128,128]{2,1,0:T(8,128)(2,1)S(1)} %get-tuple-element.101), channel_id=1, source_target_pairs={{0,16},{4,20},{8,24},{12,28},{16,0},{20,4},{24,8},{28,12},{1,17},{... | collective-permute-start | bytes 393224 | tf_op jit(solution)/shard_map/ppermute | solution.py:662
  40.6 3.3 %collective-permute-done.2.top_ref = bf16[4,128,128]{2,1,0:T(8,128)(2,1)S(1)} collective-permute-done((bf16[4,128,128]{2,1,0:T(8,128)(2,1)S(1)}, bf16[4,128,128]{2,1,0:T(8,128)(2,1)S(1)}, u32[]{:S(2)}, u32[]{:S(2)}) %collective-permute-start.2) | collective-permute-done | bytes 131104 | tf_op jit(solution)/shard_map/ppermute | solution.py:662
  46.0 2.5 %shard_map.261 = (bf16[128,2048]{1,0:T(8,128)(2,1)}, bf16[128,2048]{1,0:T(8,128)(2,1)}, bf16[128,2048]{1,0:T(8,128)(2,1)}, bf16[256,1024]{1,0:T(8,128)(2,1)S(1)}...) custom-call(s32[1]{0:T(128)} %bitcast.base_ref.here_ref._, bf16[128,2048]{1,0:T(8,128)(2,1)S(1)} %bitcast.43, ...), custom_call_target="tpu_custom_call" | custom-call | tf_op jit(solution)/shard_map/pallas_call | solution.py:838
  48.5 2.5 %shard_map.262 = (bf16[128,2048]{1,0:T(8,128)(2,1)}, bf16[128,2048]{1,0:T(8,128)(2,1)}, bf16[128,2048]{1,0:T(8,128)(2,1)}, f32[8,128,512]{2,1,0:T(8,128)S(1)}) custom-call(s32[1]{0:T(128)} %bitcast.base_ref.here_ref._, bf16[128,2048]{1,0:T(8,128)(2,1)S(1)} %bitcast.44, ...), custom_call_target="tpu_custom_call", output_to_operand_aliasing={{0}: (9, {}), {1}: (10, {}), {2}: (11, {})} | custom-call | tf_op jit(solution)/shard_map/pallas_call | solution.py:838
  51.1 2.5 %shard_map.263 = (bf16[128,2048]{1,0:T(8,128)(2,1)}, bf16[128,2048]{1,0:T(8,128)(2,1)}, bf16[128,2048]{1,0:T(8,128)(2,1)}, f32[8,128,512]{2,1,0:T(8,128)S(1)}) custom-call(s32[1]{0:T(128)} %bitcast.base_ref.here_ref._, bf16[128,2048]{1,0:T(8,128)(2,1)S(1)} %bitcast.45, ...), custom_call_target="tpu_custom_call", output_to_operand_aliasing={{0}: (9, {}), {1}: (10, {}), {2}: (11, {})} | custom-call | tf_op jit(solution)/shard_map/pallas_call | solution.py:838
  53.6 2.7 %shard_map.264 = (bf16[128,2048]{1,0:T(8,128)(2,1)}, bf16[128,2048]{1,0:T(8,128)(2,1)}, bf16[128,2048]{1,0:T(8,128)(2,1)}, f32[4,128,512]{2,1,0:T(8,128)S(1)}, bf16[4,128,512]{2,1,0:T(8,128)(2,1)S(1)}) custom-call(s32[1]{0:T(128)} %bitcast.base_ref.here_ref._, ...), custom_call_target="tpu_custom_call", output_to_operand_aliasing={{0}: (9, {}), {1}: (10, {}), {2}: (11, {})} | custom-call | tf_op jit(solution)/shard_map/pallas_call | solution.py:838
  58.5 2.0 %shard_map.250 = (bf16[528,128]{1,0:T(8,128)(2,1)S(1)}, f32[4,128,128]{2,1,0:T(8,128)S(1)}, f32[4,128,128]{2,1,0:T(8,128)S(1)}, f32[4,128,128]{2,1,0:T(8,128)S(1...) custom-call(s32[1]{0:T(128)} %bitcast.base_ref.here_ref._, ...), custom_call_target="tpu_custom_call", output_to_operand_aliasing={{7}: (13, {}), {8}: (14, {})} | custom-call | tf_op jit(solution)/shard_map/pallas_call | solution.py:641
  62.0 6.2 %collective-permute-done.4.recv_ref = bf16[528,128]{1,0:T(8,128)(2,1)S(1)} collective-permute-done((bf16[528,128]{1,0:T(8,128)(2,1)S(1)}, bf16[528,128]{1,0:T(8,128)(2,1)S(1)}, u32[]{:S(2)}, u32[]{:S(2)}) %collective-permute-start.4) | collective-permute-done | bytes 135200 | tf_op jit(solution)/shard_map/ppermute | solution.py:662
  69.3 5.0 %collective-permute-done.5.recv_ref = bf16[528,128]{1,0:T(8,128)(2,1)S(1)} collective-permute-done((bf16[528,128]{1,0:T(8,128)(2,1)S(1)}, bf16[528,128]{1,0:T(8,128)(2,1)S(1)}, u32[]{:S(2)}, u32[]{:S(2)}) %collective-permute-start.5) | collective-permute-done | bytes 135200 | tf_op jit(solution)/shard_map/ppermute | solution.py:662
  74.5 1.8 %collective-permute-start.6 = (bf16[528,128]{1,0:T(8,128)(2,1)S(1)}, bf16[528,128]{1,0:T(8,128)(2,1)S(1)}, u32[]{:S(2)}, u32[]{:S(2)}) collective-permute-start(bf16[528,128]{1,0:T(8,128)(2,1)S(1)} %get-tuple-element.131.mine_ref), channel_id=1, source_target_pairs={{0,16},{4,20},{8,24},{12,28},{16,0},{20,4},{24,8},{28,12},{1,17},{... | collective-permute-start | bytes 405512 | tf_op jit(solution)/shard_map/ppermute | solution.py:662
  76.3 4.9 %collective-permute-done.6.top_ref = bf16[528,128]{1,0:T(8,128)(2,1)S(1)} collective-permute-done((bf16[528,128]{1,0:T(8,128)(2,1)S(1)}, bf16[528,128]{1,0:T(8,128)(2,1)S(1)}, u32[]{:S(2)}, u32[]{:S(2)}) %collective-permute-start.6) | collective-permute-done | bytes 135200 | tf_op jit(solution)/shard_map/ppermute | solution.py:662
  85.6 3.6 %shard_map.251 = (f32[4,128,128]{2,1,0:T(8,128)S(1)}, f32[4,128,128]{2,1,0:T(8,128)S(1)}, f32[4,128,128]{2,1,0:T(8,128)S(1)}, f32[4,128,128]{2,1,0:T(8,128)S(1)}...) custom-call(s32[1]{0:T(128)} %bitcast.base_ref.here_ref._, ...), custom_call_target="tpu_custom_call" | custom-call | tf_op jit(solution)/shard_map/pallas_call | solution.py:641
  89.2 1.8 %shard_map.255 = (bf16[4,128,128]{2,1,0:T(8,128)(2,1)S(1)}, f32[4,128,128]{2,1,0:T(8,128)S(1)}, bf16[4,128,128]{2,1,0:T(8,128)(2,1)S(1)}, f32[128,128]{1,0:T(8,1...) custom-call(s32[1]{0:T(128)} %bitcast.base_ref.here_ref._, ...), custom_call_target="tpu_custom_call" | custom-call | tf_op jit(solution)/shard_map/pallas_call | solution.py:641
  91.0 2.1 %shard_map.256 = (bf16[4,128,128]{2,1,0:T(8,128)(2,1)S(1)}, f32[4,128,128]{2,1,0:T(8,128)S(1)}, bf16[4,128,128]{2,1,0:T(8,128)(2,1)S(1)}, f32[8,128]{1,0:T(8,128...) custom-call(s32[1]{0:T(128)} %bitcast.base_ref.here_ref._, ...), custom_call_target="tpu_custom_call", output_to_operand_aliasing={{6}: (18, {})} | custom-call | tf_op jit(solution)/shard_map/pallas_call | solution.py:641
  94.3 2.0 %collective-permute-start.10 = (f32[1,128]{1,0:T(1,128)S(1)}, f32[1,128]{1,0:T(1,128)S(1)}, u32[]{:S(2)}, u32[]{:S(2)}) collective-permute-start(f32[1,128]{1,0:T(1,128)S(1)} %slice.15), channel_id=1, source_target_pairs={{0,4},{4,0},{8,12},{12,8},{16,20},{20,16},{24,28},{28,24},{1,5},{5... | collective-permute-start | bytes 1544 | tf_op jit(solution)/shard_map/ppermute | solution.py:662
  99.3 2.6 %collective-permute-done.11 = f32[1,128]{1,0:T(1,128)S(1)} collective-permute-done((f32[1,128]{1,0:T(1,128)S(1)}, f32[1,128]{1,0:T(1,128)S(1)}, u32[]{:S(2)}, u32[]{:S(2)}) %collective-permute-start.11) | collective-permute-done | bytes 544 | tf_op jit(solution)/shard_map/ppermute | solution.py:662
  102.0 2.9 %collective-permute-start.12 = (f32[1,128]{1,0:T(1,128)S(1)}, f32[1,128]{1,0:T(1,128)S(1)}, u32[]{:S(2)}, u32[]{:S(2)}) collective-permute-start(f32[1,128]{1,0:T(1,128)S(1)} %add.27), channel_id=1, source_target_pairs={{0,16},{4,20},{8,24},{12,28},{16,0},{20,4},{24,8},{28,12},{1,17},{... | collective-permute-start | bytes 1544 | tf_op jit(solution)/shard_map/ppermute | solution.py:662
  106.6 3.0 %collective-permute-start.18 = (bf16[1,128,512]{2,1,0:T(8,128)(2,1)S(1)}, bf16[1,128,512]{2,1,0:T(8,128)(2,1)S(1)}, u32[]{:S(2)}, u32[]{:S(2)}) collective-permute-start(bf16[1,128,512]{2,1,0:T(8,128)(2,1)S(1)} %split.31), channel_id=1, source_target_pairs={{0,16},{4,20},{8,24},{12,28},{16,0},{20,4},{24,8},{28,12},{1,17},{... | collective-permute-start | bytes 393224 | tf_op jit(solution)/shard_map/ppermute | solution.py:662
  110.1 3.8 %collective-permute-done.18 = bf16[1,128,512]{2,1,0:T(8,128)(2,1)S(1)} collective-permute-done((bf16[1,128,512]{2,1,0:T(8,128)(2,1)S(1)}, bf16[1,128,512]{2,1,0:T(8,128)(2,1)S(1)}, u32[]{:S(2)}, u32[]{:S(2)}) %collective-permute-start.18) | collective-permute-done | bytes 131104 | tf_op jit(solution)/shard_map/ppermute | solution.py:662
  (69 shorter events, 24.2 us)
Async XLA Ops:
  1.5 10.4 %collective-permute-start.13 = (bf16[1,128,512]{2,1,0:T(8,128)(2,1)S(1)}, bf16[1,128,512]{2,1,0:T(8,128)(2,1)S(1)}, u32[]{:S(2)}, u32[]{:S(2)}) collective-permute-start(bf16[1,128,512]{2,1,0:T(8,128)(2,1)S(1)} %shard_map.258.first_ref), channel_id=1, source_target_pairs={{0,16},{4,20},{8,24},{12,28},{16,0},{20,4},{24,8},{28,12},{1,17},{... | collective-permute-start | bytes 393224 | tf_op jit(solution)/shard_map/ppermute | solution.py:662
  12.0 34.0 %copy-start = (bf16[1,128,2048]{2,1,0:T(8,128)(2,1)S(1)}, bf16[1,128,2048]{2,1,0:T(8,128)(2,1)}, u32[]{:S(2)}) copy-start(bf16[1,128,2048]{2,1,0:T(8,128)(2,1)} %param.23) | copy-start | bytes 1572868
  12.0 33.9 %copy-start.1 = (bf16[1,128,2048]{2,1,0:T(8,128)(2,1)S(1)}, bf16[1,128,2048]{2,1,0:T(8,128)(2,1)}, u32[]{:S(2)}) copy-start(bf16[1,128,2048]{2,1,0:T(8,128)(2,1)} %param.26) | copy-start | bytes 1572868
  12.0 33.9 %copy-start.2 = (bf16[1,128,2048]{2,1,0:T(8,128)(2,1)S(1)}, bf16[1,128,2048]{2,1,0:T(8,128)(2,1)}, u32[]{:S(2)}) copy-start(bf16[1,128,2048]{2,1,0:T(8,128)(2,1)} %param.27) | copy-start | bytes 1572868
  12.0 9.1 %collective-permute-start.14 = (bf16[2,128,512]{2,1,0:T(8,128)(2,1)S(1)}, bf16[2,128,512]{2,1,0:T(8,128)(2,1)S(1)}, u32[]{:S(2)}, u32[]{:S(2)}) collective-permute-start(bf16[2,128,512]{2,1,0:T(8,128)(2,1)S(1)} %shard_map.259.first_ref), channel_id=1, source_target_pairs={{0,8},{4,12},{8,0},{12,4},{16,24},{20,28},{24,16},{28,20},{1,9},{5... | collective-permute-start | bytes 786440 | tf_op jit(solution)/shard_map/ppermute | solution.py:662
  19.6 9.2 %collective-permute-start = (bf16[4,128,256]{2,1,0:T(8,128)(2,1)S(1)}, bf16[4,128,256]{2,1,0:T(8,128)(2,1)S(1)}, u32[]{:S(2)}, u32[]{:S(2)}) collective-permute-start(bf16[4,128,256]{2,1,0:T(8,128)(2,1)S(1)} %get-tuple-element.99), channel_id=1, source_target_pairs={{0,4},{4,0},{8,12},{12,8},{16,20},{20,16},{24,28},{28,24},{1,5},{5... | collective-permute-start | bytes 786440 | tf_op jit(solution)/shard_map/ppermute | solution.py:662
  21.2 24.8 %collective-permute-start.15 = (bf16[4,128,512]{2,1,0:T(8,128)(2,1)S(1)}, bf16[4,128,512]{2,1,0:T(8,128)(2,1)S(1)}, u32[]{:S(2)}, u32[]{:S(2)}) collective-permute-start(bf16[4,128,512]{2,1,0:T(8,128)(2,1)S(1)} %shard_map.260.near_ref), channel_id=1, source_target_pairs={{0,4},{4,0},{8,12},{12,8},{16,20},{20,16},{24,28},{28,24},{1,5},{5... | collective-permute-start | bytes 1572872 | tf_op jit(solution)/shard_map/ppermute | solution.py:662
  29.1 6.4 %collective-permute-start.1 = (bf16[4,128,256]{2,1,0:T(8,128)(2,1)S(1)}, bf16[4,128,256]{2,1,0:T(8,128)(2,1)S(1)}, u32[]{:S(2)}, u32[]{:S(2)}) collective-permute-start(bf16[4,128,256]{2,1,0:T(8,128)(2,1)S(1)} %get-tuple-element.100.own_ref), channel_id=1, source_target_pairs={{0,8},{4,12},{8,0},{12,4},{16,24},{20,28},{24,16},{28,20},{1,9},{5... | collective-permute-start | bytes 786440 | tf_op jit(solution)/shard_map/ppermute | solution.py:662
  35.8 8.2 %collective-permute-start.2 = (bf16[4,128,128]{2,1,0:T(8,128)(2,1)S(1)}, bf16[4,128,128]{2,1,0:T(8,128)(2,1)S(1)}, u32[]{:S(2)}, u32[]{:S(2)}) collective-permute-start(bf16[4,128,128]{2,1,0:T(8,128)(2,1)S(1)} %get-tuple-element.101), channel_id=1, source_target_pairs={{0,16},{4,20},{8,24},{12,28},{16,0},{20,4},{24,8},{28,12},{1,17},{... | collective-permute-start | bytes 393224 | tf_op jit(solution)/shard_map/ppermute | solution.py:662
  44.4 14.1 %collective-permute-start.3 = (bf16[4,128,128]{2,1,0:T(8,128)(2,1)S(1)}, bf16[4,128,128]{2,1,0:T(8,128)(2,1)S(1)}, u32[]{:S(2)}, u32[]{:S(2)}) collective-permute-start(bf16[4,128,128]{2,1,0:T(8,128)(2,1)S(1)} %get-tuple-element.104), channel_id=1, source_target_pairs={{0,4},{4,0},{8,12},{12,8},{16,20},{20,16},{24,28},{28,24},{1,5},{5... | collective-permute-start | bytes 393224 | tf_op jit(solution)/shard_map/ppermute | solution.py:662
  56.4 26.5 %collective-permute-start.16 = (bf16[4,128,512]{2,1,0:T(8,128)(2,1)S(1)}, bf16[4,128,512]{2,1,0:T(8,128)(2,1)S(1)}, u32[]{:S(2)}, u32[]{:S(2)}) collective-permute-start(bf16[4,128,512]{2,1,0:T(8,128)(2,1)S(1)} %get-tuple-element.180), channel_id=1, source_target_pairs={{0,4},{4,0},{8,12},{12,8},{16,20},{20,16},{24,28},{28,24},{1,5},{5... | collective-permute-start | bytes 1572872 | tf_op jit(solution)/shard_map/ppermute | solution.py:662
  60.5 7.7 %collective-permute-start.4 = (bf16[528,128]{1,0:T(8,128)(2,1)S(1)}, bf16[528,128]{1,0:T(8,128)(2,1)S(1)}, u32[]{:S(2)}, u32[]{:S(2)}) collective-permute-start(bf16[528,128]{1,0:T(8,128)(2,1)S(1)} %get-tuple-element.129.mine_ref), channel_id=1, source_target_pairs={{0,4},{4,0},{8,12},{12,8},{16,20},{20,16},{24,28},{28,24},{1,5},{5... | collective-permute-start | bytes 405512 | tf_op jit(solution)/shard_map/ppermute | solution.py:662
  68.5 5.8 %collective-permute-start.5 = (bf16[528,128]{1,0:T(8,128)(2,1)S(1)}, bf16[528,128]{1,0:T(8,128)(2,1)S(1)}, u32[]{:S(2)}, u32[]{:S(2)}) collective-permute-start(bf16[528,128]{1,0:T(8,128)(2,1)S(1)} %get-tuple-element.130.own_ref.mine_ref), channel_id=1, source_target_pairs={{0,8},{4,12},{8,0},{12,4},{16,24},{20,28},{24,16},{28,20},{1,9},{5... | collective-permute-start | bytes 405512 | tf_op jit(solution)/shard_map/ppermute | solution.py:662
  74.5 6.7 %collective-permute-start.6 = (bf16[528,128]{1,0:T(8,128)(2,1)S(1)}, bf16[528,128]{1,0:T(8,128)(2,1)S(1)}, u32[]{:S(2)}, u32[]{:S(2)}) collective-permute-start(bf16[528,128]{1,0:T(8,128)(2,1)S(1)} %get-tuple-element.131.mine_ref), channel_id=1, source_target_pairs={{0,16},{4,20},{8,24},{12,28},{16,0},{20,4},{24,8},{28,12},{1,17},{... | collective-permute-start | bytes 405512 | tf_op jit(solution)/shard_map/ppermute | solution.py:662
  81.2 4.4 %copy-start.5 = (bf16[1,128,1024]{2,1,0:T(8,128)(2,1)S(1)}, bf16[1,128,1024]{2,1,0:T(8,128)(2,1)}, u32[]{:S(2)}) copy-start(bf16[1,128,1024]{2,1,0:T(8,128)(2,1)} %param.14) | copy-start | bytes 786436
  81.6 9.3 %collective-permute-start.7 = (bf16[4,128,128]{2,1,0:T(8,128)(2,1)S(1)}, bf16[4,128,128]{2,1,0:T(8,128)(2,1)S(1)}, u32[]{:S(2)}, u32[]{:S(2)}) collective-permute-start(bf16[4,128,128]{2,1,0:T(8,128)(2,1)S(1)} %get-tuple-element.145), channel_id=1, source_target_pairs={{0,4},{4,0},{8,12},{12,8},{16,20},{20,16},{24,28},{28,24},{1,5},{5... | collective-permute-start | bytes 393224 | tf_op jit(solution)/shard_map/ppermute | solution.py:662
  83.0 6.2 %copy-start.4 = (bf16[1,128,1024]{2,1,0:T(8,128)(2,1)S(1)}, bf16[1,128,1024]{2,1,0:T(8,128)(2,1)}, u32[]{:S(2)}) copy-start(bf16[1,128,1024]{2,1,0:T(8,128)(2,1)} %param.15) | copy-start | bytes 786436
  83.1 23.4 %collective-permute-start.17 = (bf16[2,128,512]{2,1,0:T(8,128)(2,1)S(1)}, bf16[2,128,512]{2,1,0:T(8,128)(2,1)S(1)}, u32[]{:S(2)}, u32[]{:S(2)}) collective-permute-start(bf16[2,128,512]{2,1,0:T(8,128)(2,1)S(1)} %split.30), channel_id=1, source_target_pairs={{0,8},{4,12},{8,0},{12,4},{16,24},{20,28},{24,16},{28,20},{1,9},{5... | collective-permute-start | bytes 786440 | tf_op jit(solution)/shard_map/ppermute | solution.py:662
  84.1 6.9 %collective-permute-start.8 = (f32[1,128]{1,0:T(1,128)S(1)}, f32[1,128]{1,0:T(1,128)S(1)}, u32[]{:S(2)}, u32[]{:S(2)}) collective-permute-start(f32[1,128]{1,0:T(1,128)S(1)} %get-tuple-element.153), channel_id=1, source_target_pairs={{0,2},{2,0},{1,3},{3,1},{4,6},{6,4},{5,7},{7,5},{8,10},{10,8},{9,1... | collective-permute-start | bytes 1544 | tf_op jit(solution)/shard_map/ppermute | solution.py:662
  93.1 1.2 %collective-permute-start.9 = (f32[2,128]{1,0:T(2,128)S(1)}, f32[2,128]{1,0:T(2,128)S(1)}, u32[]{:S(2)}, u32[]{:S(2)}) collective-permute-start(f32[2,128]{1,0:T(2,128)S(1)} %get-tuple-element.161), channel_id=1, source_target_pairs={{0,1},{1,0},{2,3},{3,2},{4,5},{5,4},{6,7},{7,6},{8,9},{9,8},{10,11... | collective-permute-start | bytes 3080 | tf_op jit(solution)/shard_map/ppermute | solution.py:662
  94.3 3.6 %collective-permute-start.10 = (f32[1,128]{1,0:T(1,128)S(1)}, f32[1,128]{1,0:T(1,128)S(1)}, u32[]{:S(2)}, u32[]{:S(2)}) collective-permute-start(f32[1,128]{1,0:T(1,128)S(1)} %slice.15), channel_id=1, source_target_pairs={{0,4},{4,0},{8,12},{12,8},{16,20},{20,16},{24,28},{28,24},{1,5},{5... | collective-permute-start | bytes 1544 | tf_op jit(solution)/shard_map/ppermute | solution.py:662
  98.4 3.6 %collective-permute-start.11 = (f32[1,128]{1,0:T(1,128)S(1)}, f32[1,128]{1,0:T(1,128)S(1)}, u32[]{:S(2)}, u32[]{:S(2)}) collective-permute-start(f32[1,128]{1,0:T(1,128)S(1)} %get-tuple-element.185), channel_id=1, source_target_pairs={{0,8},{4,12},{8,0},{12,4},{16,24},{20,28},{24,16},{28,20},{1,9},{5... | collective-permute-start | bytes 1544 | tf_op jit(solution)/shard_map/ppermute | solution.py:662
  102.0 4.5 %collective-permute-start.12 = (f32[1,128]{1,0:T(1,128)S(1)}, f32[1,128]{1,0:T(1,128)S(1)}, u32[]{:S(2)}, u32[]{:S(2)}) collective-permute-start(f32[1,128]{1,0:T(1,128)S(1)} %add.27), channel_id=1, source_target_pairs={{0,16},{4,20},{8,24},{12,28},{16,0},{20,4},{24,8},{28,12},{1,17},{... | collective-permute-start | bytes 1544 | tf_op jit(solution)/shard_map/ppermute | solution.py:662
  106.6 7.3 %collective-permute-start.18 = (bf16[1,128,512]{2,1,0:T(8,128)(2,1)S(1)}, bf16[1,128,512]{2,1,0:T(8,128)(2,1)S(1)}, u32[]{:S(2)}, u32[]{:S(2)}) collective-permute-start(bf16[1,128,512]{2,1,0:T(8,128)(2,1)S(1)} %split.31), channel_id=1, source_target_pairs={{0,16},{4,20},{8,24},{12,28},{16,0},{20,4},{24,8},{28,12},{1,17},{... | collective-permute-start | bytes 393224 | tf_op jit(solution)/shard_map/ppermute | solution.py:662
  (6 other events, 16.6 us)
where the time goes:
time: 115 us
  waiting for transfers between devices  47.1 us (41%)
  Pallas kernels  32.6 us (28%)
  starting transfers between devices  32 us (28%)
  local copies, waits for them, and re-layouts  1.28 us (1%)
    ppermute x19, waiting for transfers between devices, swap(): return lax.ppermute(value, axis, [(i, i ^ offset) for i in range(count)])  47.1 us
    ppermute x19, starting transfers between devices, swap(): return lax.ppermute(value, axis, [(i, i ^ offset) for i in range(count)])  32 us
    pallas_call x16, Pallas kernels, call(): pl.pallas_call(kernel, out_shape=tuple((jax.ShapeDtypeStruct(shape, dtype...  22.2 us
    pallas_call x4, Pallas kernels, per_device(): pl.pallas_call(functools.partial(attention_kernel, offsets, start, end),...  10.4 us
  transfers between devices with their start and end apart: 19, of which 11 were waited for; matrix products, arithmetic and copies ran while one was open for 1% of the time, Pallas kernels for 28%

commit v1 on v0

--- a/solution.py
+++ b/solution.py
@@ -21,7 +21,7 @@
 DX = F32
 GDX = F32
 MK = F32
-OUTER = F32
+OUTER = BF
 VMEM_LIMIT = 20 << 20
 
 
@@ -108,17 +108,17 @@
 
 
 def prepare_kernel(heads, base_ref, *refs):
-    sources, refs = refs[:6], refs[6:]
-    inputs, sems = refs[15:21], refs[21]
+    sources, refs = refs[:5], refs[5:]
+    inputs, sems = refs[11:16], refs[16]
     copies = fetch(sources, inputs, sems)
-    q_ref, k_ref, v_ref, beta_ref, decay_ref, log_ref = inputs
-    refs = refs[:15]
+    k_ref, v_ref, beta_ref, decay_ref, log_ref = inputs
+    refs = refs[:11]
     half = heads // 2
     base = (base_ref[0] & 1) * (heads // 2)
-    g_ref, b_ref, pad = refs[12:]
+    g_ref, b_ref, pad = refs[8:]
     perm = slot_matrix(base, heads, pad.shape[0])
     pad[...] = jnp.zeros_like(pad)
-    for copy in copies[3:]:
+    for copy in copies[2:]:
         copy.wait()
     pad[:heads, :] = sigmoid(beta_ref[...])
     b_ref[...] = dot(pad[...], perm, 0, 0, precision=HIGHEST)
@@ -136,26 +136,21 @@
     identity = jnp.where(row == col, 1.0, 0.0).astype(F32)
     small = 16
     copies[0].wait()
-    copies[1].wait()
     units, lowers, inverses = [], [], []
 
     def begin(s):
-        _, kb_ref, qb_ref, _, p_ref, n_ref = refs[6 * (s // half) : 6 * (s // half) + 6]
+        _, kb_ref, _, n_ref = refs[4 * (s // half) : 4 * (s // half) + 4]
         i = s % half
         cols = head_cols(base, s, size)
-        unit_q = unit_of(q_ref[:, cols].astype(F32))[0] * (size**-0.5)
         unit_k = unit_of(k_ref[:, cols].astype(F32))[0]
-        qb = unit_q.astype(KQ)
         kb = unit_k.astype(KQ)
-        qb_ref[i] = qb
         kb_ref[i] = kb
         yield
         fade = jnp.exp(jnp.where(within, g_all[:, s : s + 1] - g_rows[s : s + 1, :], 0.0))
-        both = dot(jnp.concatenate([kb, qb], 0), kb, 1, 1)
-        yield
-        plain = jnp.where(strict, fade * both[:rows], 0.0)
+        both = dot(kb, kb, 1, 1)
+        yield
+        plain = jnp.where(strict, fade * both, 0.0)
         n_ref[i] = plain.astype(n_ref.dtype)
-        p_ref[i] = jnp.where(within, fade * both[rows:], 0.0).astype(SCO)
         lower = betas[:, s : s + 1] * plain
         lowers.append(lower)
         diag = jnp.where((row // small) == (col // small), lower, 0.0)
@@ -175,10 +170,10 @@
         inverses = [x - mm3(x, y) for x, y in zip(inverses, inner)]
         span *= 2
     row_k, col_k = ids(size, size)
-    copies[2].wait()
+    copies[1].wait()
 
     def finish(s):
-        maps_ref, kb_ref, _, m_ref, _, _ = refs[6 * (s // half) : 6 * (s // half) + 6]
+        maps_ref, kb_ref, m_ref, _ = refs[4 * (s // half) : 4 * (s // half) + 4]
         i = s % half
         cols = head_cols(base, s, size)
         gc = g_all[:, s : s + 1]
@@ -199,6 +194,32 @@
         maps_ref[i] = jnp.concatenate([carry, both[:, size:]], 1).astype(BF)
 
     interleave(finish(s) for s in range(heads))
+
+
+def score_kernel(heads, base_ref, q_ref, g_ref, *refs):
+    half = heads // 2
+    base = (base_ref[0] & 1) * half
+    rows = g_ref.shape[0]
+    size = refs[0].shape[2]
+    row, col = ids(rows, rows)
+    within = row >= col
+    g_all = g_ref[...]
+    g_rows = g_all.T
+
+    def one(s):
+        i, side = s % half, s // half
+        kb = refs[side][i]
+        qb_ref, p_ref = refs[2 + 2 * side : 4 + 2 * side]
+        cols = head_cols(base, s, size)
+        qb = (unit_of(q_ref[:, cols].astype(F32))[0] * (size**-0.5)).astype(KQ)
+        qb_ref[i] = qb
+        yield
+        fade = jnp.exp(jnp.where(within, g_all[:, s : s + 1] - g_rows[s : s + 1, :], 0.0))
+        products = dot(qb, kb, 1, 1)
+        yield
+        p_ref[i] = jnp.where(within, fade * products, 0.0).astype(SCO)
+
+    interleave(one(s) for s in range(heads))
 
 
 def precise(carry, state, ca=1):
@@ -538,6 +559,28 @@
     cut = first_ref.shape[0]
     out_ref[:cut] = first_ref[...]
     out_ref[cut:] = second_ref[...]
+
+
+def end_kernel(_, sums_ref, moved_ref, *refs):
+    log_ref, gain_ref = refs[-2:]
+    count = log_ref.shape[1]
+    log_ref[...] = sums_ref[0:1, :count] + moved_ref[0:1, :count]
+    gain = sums_ref[1:2, :]
+    for ref in refs[:-2]:
+        gain = gain + ref[1:2, :]
+    gain_ref[...] = gain
+
+
+def half_sum_kernel(parts, _, own_ref, moved_ref, keep_ref, send_ref):
+    keep_ref[...] = own_ref[:parts] + moved_ref[:parts].astype(F32)
+    send_ref[...] = (own_ref[parts:] + moved_ref[parts:].astype(F32)).astype(BF)
+
+
+def last_sum_kernel(_, own_ref, moved_ref, key_ref, value_ref):
+    total = own_ref[0] + moved_ref[0].astype(F32)
+    cut = key_ref.shape[1]
+    key_ref[...] = total[:, :cut].astype(BF)
+    value_ref[...] = total[:, cut:].astype(BF)
 
 
 def attention_kernel(offsets, start, end, here_ref, q_ref, gate_ref, cot_ref, near_ref, far_ref, *refs):
@@ -728,17 +771,23 @@
     packed = ((half * size + 16, size), BF)
     column_scratch = pltpu.VMEM(*column)
 
-    kept = [maps, (cube[0], KQ), (cube[0], KQ), (square[0], INV), (square[0], SCO), (square[0], SCO)]
+    kept = [maps, (cube[0], KQ), (square[0], INV), (square[0], SCO)]
     results = call(
         functools.partial(prepare_kernel, heads), kept + kept + [column, column],
         [pltpu.VMEM(*turned)]
-        + [pltpu.VMEM(x.shape, x.dtype) for x in (q, k, v, beta, decay, logs)]
-        + [pltpu.SemaphoreType.DMA((6,))],
-        spot, q, k, v, beta, decay, logs, far=True,
-    )
-    keep, *near = results[:6]
-    send, *far = results[6:12]
-    g, b = results[12:]
+        + [pltpu.VMEM(x.shape, x.dtype) for x in (k, v, beta, decay, logs)]
+        + [pltpu.SemaphoreType.DMA((5,))],
+        spot, k, v, beta, decay, logs, far=True,
+    )
+    keep, kb_near, m_near, n_near = results[:4]
+    send, kb_far, m_far, n_far = results[4:8]
+    g, b = results[8:]
+    qb_near, p_near, qb_far, p_far = call(
+        functools.partial(score_kernel, heads), [(cube[0], KQ), (square[0], SCO)] * 2, [],
+        spot, q, g, kb_near, kb_far,
+    )
+    near = [kb_near, qb_near, m_near, p_near, n_near]
+    far = [kb_far, qb_far, m_far, p_far, n_far]
     pairs = []
     for level in range(levels - 1):
         moved = swap(send, "ctx", 1 << level)
@@ -783,7 +832,6 @@
         spot, keep, moved, *pairs, *locals_,
     )
     far_grad = swap(send, "ctx", 1)
-    gain_part = axis_sum(gain_part, "head")
     dkp_near, mk_near, dkp_far, mk_far, dgc, dgr, dq = call(
         functools.partial(query_kernel, heads),
         [cube_wide, (cube[0], MK), cube_wide, (cube[0], MK), column, turned, flat], [], spot, q, g,
@@ -811,10 +859,18 @@
         far_state, far[0], dkp_far, gdv_far, dmat_far, dtail_far,
     )
     sums = axis_sum(sums, "section")
-    gain_grad = sums[1]
-    log_grad = sums[:1]
-    for level in range(levels):
-        log_grad = log_grad + swap(log_grad, "ctx", 1 << level)
+    offset, partner = 1, []
+    while offset < lax.axis_size("head"):
+        partner.append(swap(sums, "head", offset))
+        offset *= 2
+    summed = lax.broadcasted_iota(jnp.int32, sums.shape, 0) == 0
+    for level in range(levels - 1):
+        moved = swap(sums, "ctx", 1 << level)
+        sums = sums + jnp.where(summed, moved, 0.0)
+    moved = swap(sums, "ctx", 1 << (levels - 1))
+    log_grad, gain_grad = call(
+        end_kernel, [((1, heads), F32), ((1, size), F32)], [], spot, sums, moved, *partner
+    )
 
     groups = attn_query.shape[2] // AD
     group = 2 if groups % 2 == 0 else 1
@@ -857,16 +913,21 @@
         extra = [keys_t, values_t, results[-1]]
     attn_out, dquery, dgate_att = outs
     own, send = results[-2:]
-    moved = swap(send, "ctx", 1)
-    own = own + moved.astype(F32)
-    jump = 2
+    jump = 1
     while jump < count:
-        own, send = jnp.split(own, 2)
-        send = send.astype(BF)
         moved = swap(send, "ctx", jump)
-        own = own + moved.astype(F32)
+        parts = own.shape[0] // 2
+        if parts:
+            own, send = call(
+                functools.partial(half_sum_kernel, parts),
+                [((parts,) + own.shape[1:], F32), ((parts,) + own.shape[1:], BF)], [],
+                spot, own, moved,
+            )
+        else:
+            dkey, dvalue = call(
+                last_sum_kernel, [((rows_att, key_width), BF)] * 2, [], spot, own, moved
+            )
         jump *= 2
-    own = own[0].astype(BF)
     return (
         out[None],
         dq[None],
@@ -874,13 +935,13 @@
         dv[None],
         dbeta.T[None],
         ddecay.T[None],
-        log_grad[0, :heads],
-        gain_grad,
+        log_grad[0],
+        gain_grad[0],
         dgate[None],
         attn_out[None],
         dquery[None],
-        own[:, :key_width][None],
-        own[:, key_width:][None],
+        dkey[None],
+        dvalue[None],
         dgate_att[None],
     )
 

time: 115 us -> 96.6 us (0.84)
  waiting for transfers between devices: 47.1 us -> 36.1 us
  starting transfers between devices: 32 us -> 24.8 us
  Pallas kernels: 32.6 us -> 34.5 us
  local copies, waits for them, and re-layouts: 1.28 us -> 0.06 us
    ppermute x19, waiting for transfers between devices: 47.1 us -> 36.1 us  [swap(): return lax.ppermute(value, axis, [(i, i ^ offset) for i in range(count)])]
    ppermute x19, starting transfers between devices: 32 us -> 24.8 us  [swap(): return lax.ppermute(value, axis, [(i, i ^ offset) for i in range(count)])]
    pallas_call x16 -> x21, Pallas kernels: 22.2 us -> 24.1 us  [call(): pl.pallas_call(kernel, out_shape=tuple((jax.ShapeDtypeStruct(shape, dtype...]
  transfers between devices with their start and end apart: 19 -> 19, of which waited for: 11 -> 10; matrix products, arithmetic and copies ran while one was open for 1% -> 0% of each run, Pallas kernels for 28% -> 34%
where the time goes in v1:
time: 96.6 us; the launch traced here: 96.4 us
  waiting for transfers between devices  36.1 us (37%)
  Pallas kernels  34.5 us (36%)
  starting transfers between devices  24.8 us (26%)
    ppermute x19, waiting for transfers between devices, swap(): return lax.ppermute(value, axis, [(i, i ^ offset) for i in range(count)])  36.1 us
    ppermute x19, starting transfers between devices, swap(): return lax.ppermute(value, axis, [(i, i ^ offset) for i in range(count)])  24.8 us
    pallas_call x21, Pallas kernels, call(): pl.pallas_call(kernel, out_shape=tuple((jax.ShapeDtypeStruct(shape, dtype...  24.1 us
    pallas_call x4, Pallas kernels, per_device(): pl.pallas_call(functools.partial(attention_kernel, offsets, start, end),...  10.4 us
  transfers between devices with their start and end apart: 19, of which 10 were waited for; matrix products, arithmetic and copies ran while one was open for 0% of the time, Pallas kernels for 34%

profile of v1, /device:TPU:0, one launch (start us, length us, event | category | flops | bytes accessed | tf_op | source)
XLA Modules:
  0.0 96.4 jit_solution(14654948637369622208)
XLA Ops:
  1.5 4.1 %collective-permute-start.13 = (bf16[1,128,512]{2,1,0:T(8,128)(2,1)S(1)}, bf16[1,128,512]{2,1,0:T(8,128)(2,1)S(1)}, u32[]{:S(2)}, u32[]{:S(2)}) collective-permute-start(bf16[1,128,512]{2,1,0:T(8,128)(2,1)S(1)} %shard_map.260.first_ref), channel_id=1, source_target_pairs={{0,16},{4,20},{8,24},{12,28},{16,0},{20,4},{24,8},{28,12},{1,17},{... | collective-permute-start | bytes 393224 | tf_op jit(solution)/shard_map/ppermute | solution.py:705
  5.7 6.0 %shard_map.245 = (bf16[4,128,256]{2,1,0:T(8,128)(2,1)S(1)}, f32[4,128,128]{2,1,0:T(8,128)S(1)}, f32[4,128,128]{2,1,0:T(8,128)S(1)}, f32[4,128,128]{2,1,0:T(8,128...) custom-call(s32[1]{0:T(128)} %bitcast.base_ref.here_ref._, ...), custom_call_target="tpu_custom_call" | custom-call | tf_op jit(solution)/shard_map/pallas_call | solution.py:684
  13.4 1.6 %collective-permute-start.14 = (bf16[2,128,512]{2,1,0:T(8,128)(2,1)S(1)}, bf16[2,128,512]{2,1,0:T(8,128)(2,1)S(1)}, u32[]{:S(2)}, u32[]{:S(2)}) collective-permute-start(bf16[2,128,512]{2,1,0:T(8,128)(2,1)S(1)} %shard_map.261.first_ref), channel_id=1, source_target_pairs={{0,8},{4,12},{8,0},{12,4},{16,24},{20,28},{24,16},{28,20},{1,9},{5... | collective-permute-start | bytes 786440 | tf_op jit(solution)/shard_map/ppermute | solution.py:705
  15.0 4.5 %collective-permute-done.recv_ref = bf16[4,128,256]{2,1,0:T(8,128)(2,1)S(1)} collective-permute-done((bf16[4,128,256]{2,1,0:T(8,128)(2,1)S(1)}, bf16[4,128,256]{2,1,0:T(8,128)(2,1)S(1)}, u32[]{:S(2)}, u32[]{:S(2)}) %collective-permute-start) | collective-permute-done | bytes 262176 | tf_op jit(solution)/shard_map/ppermute | solution.py:705
  19.9 1.6 %collective-permute-start.1 = (bf16[4,128,256]{2,1,0:T(8,128)(2,1)S(1)}, bf16[4,128,256]{2,1,0:T(8,128)(2,1)S(1)}, u32[]{:S(2)}, u32[]{:S(2)}) collective-permute-start(bf16[4,128,256]{2,1,0:T(8,128)(2,1)S(1)} %get-tuple-element.108.own_ref), channel_id=1, source_target_pairs={{0,8},{4,12},{8,0},{12,4},{16,24},{20,28},{24,16},{28,20},{1,9},{5... | collective-permute-start | bytes 786440 | tf_op jit(solution)/shard_map/ppermute | solution.py:705
  23.1 3.7 %collective-permute-done.1.recv_ref = bf16[4,128,256]{2,1,0:T(8,128)(2,1)S(1)} collective-permute-done((bf16[4,128,256]{2,1,0:T(8,128)(2,1)S(1)}, bf16[4,128,256]{2,1,0:T(8,128)(2,1)S(1)}, u32[]{:S(2)}, u32[]{:S(2)}) %collective-permute-start.1) | collective-permute-done | bytes 262176 | tf_op jit(solution)/shard_map/ppermute | solution.py:705
  28.6 5.8 %collective-permute-done.2.top_ref = bf16[4,128,128]{2,1,0:T(8,128)(2,1)S(1)} collective-permute-done((bf16[4,128,128]{2,1,0:T(8,128)(2,1)S(1)}, bf16[4,128,128]{2,1,0:T(8,128)(2,1)S(1)}, u32[]{:S(2)}, u32[]{:S(2)}) %collective-permute-start.2) | collective-permute-done | bytes 131104 | tf_op jit(solution)/shard_map/ppermute | solution.py:705
  37.1 2.2 %shard_map.250 = (bf16[528,128]{1,0:T(8,128)(2,1)S(1)}, f32[4,128,128]{2,1,0:T(8,128)S(1)}, f32[4,128,128]{2,1,0:T(8,128)S(1)}, f32[4,128,128]{2,1,0:T(8,128)S(1...) custom-call(s32[1]{0:T(128)} %bitcast.base_ref.here_ref._, ...), custom_call_target="tpu_custom_call" | custom-call | tf_op jit(solution)/shard_map/pallas_call | solution.py:684
  39.8 2.2 %shard_map.251 = (bf16[528,128]{1,0:T(8,128)(2,1)S(1)}, f32[4,128,128]{2,1,0:T(8,128)S(1)}, f32[4,128,128]{2,1,0:T(8,128)S(1)}, f32[4,128,128]{2,1,0:T(8,128)S(1...) custom-call(s32[1]{0:T(128)} %bitcast.base_ref.here_ref._, ...), custom_call_target="tpu_custom_call", output_to_operand_aliasing={{7}: (13, {}), {8}: (14, {})} | custom-call | tf_op jit(solution)/shard_map/pallas_call | solution.py:684
  43.6 2.5 %shard_map.263 = (bf16[128,2048]{1,0:T(8,128)(2,1)}, bf16[128,2048]{1,0:T(8,128)(2,1)}, bf16[128,2048]{1,0:T(8,128)(2,1)}, bf16[256,1024]{1,0:T(8,128)(2,1)S(1)}...) custom-call(s32[1]{0:T(128)} %bitcast.base_ref.here_ref._, bf16[128,2048]{1,0:T(8,128)(2,1)S(1)} %bitcast.37, ...), custom_call_target="tpu_custom_call" | custom-call | tf_op jit(solution)/shard_map/pallas_call | solution.py:894
  46.1 2.7 %shard_map.264 = (bf16[128,2048]{1,0:T(8,128)(2,1)}, bf16[128,2048]{1,0:T(8,128)(2,1)}, bf16[128,2048]{1,0:T(8,128)(2,1)}, f32[8,128,512]{2,1,0:T(8,128)S(1)}) custom-call(s32[1]{0:T(128)} %bitcast.base_ref.here_ref._, bf16[128,2048]{1,0:T(8,128)(2,1)S(1)} %bitcast.38, ...), custom_call_target="tpu_custom_call", output_to_operand_aliasing={{0}: (9, {}), {1}: (10, {}), {2}: (11, {})} | custom-call | tf_op jit(solution)/shard_map/pallas_call | solution.py:894
  48.8 2.5 %shard_map.265 = (bf16[128,2048]{1,0:T(8,128)(2,1)}, bf16[128,2048]{1,0:T(8,128)(2,1)}, bf16[128,2048]{1,0:T(8,128)(2,1)}, f32[8,128,512]{2,1,0:T(8,128)S(1)}) custom-call(s32[1]{0:T(128)} %bitcast.base_ref.here_ref._, bf16[128,2048]{1,0:T(8,128)(2,1)S(1)} %bitcast.39, ...), custom_call_target="tpu_custom_call", output_to_operand_aliasing={{0}: (9, {}), {1}: (10, {}), {2}: (11, {})} | custom-call | tf_op jit(solution)/shard_map/pallas_call | solution.py:894
  51.4 2.5 %shard_map.266 = (bf16[128,2048]{1,0:T(8,128)(2,1)}, bf16[128,2048]{1,0:T(8,128)(2,1)}, bf16[128,2048]{1,0:T(8,128)(2,1)}, f32[4,128,512]{2,1,0:T(8,128)S(1)}, bf16[4,128,512]{2,1,0:T(8,128)(2,1)S(1)}) custom-call(s32[1]{0:T(128)} %bitcast.base_ref.here_ref._, ...), custom_call_target="tpu_custom_call", output_to_operand_aliasing={{0}: (9, {}), {1}: (10, {}), {2}: (11, {})} | custom-call | tf_op jit(solution)/shard_map/pallas_call | solution.py:894
  55.2 4.6 %collective-permute-done.5.recv_ref = bf16[528,128]{1,0:T(8,128)(2,1)S(1)} collective-permute-done((bf16[528,128]{1,0:T(8,128)(2,1)S(1)}, bf16[528,128]{1,0:T(8,128)(2,1)S(1)}, u32[]{:S(2)}, u32[]{:S(2)}) %collective-permute-start.5) | collective-permute-done | bytes 135200 | tf_op jit(solution)/shard_map/ppermute | solution.py:705
  60.0 1.9 %collective-permute-start.6 = (bf16[528,128]{1,0:T(8,128)(2,1)S(1)}, bf16[528,128]{1,0:T(8,128)(2,1)S(1)}, u32[]{:S(2)}, u32[]{:S(2)}) collective-permute-start(bf16[528,128]{1,0:T(8,128)(2,1)S(1)} %get-tuple-element.139.mine_ref), channel_id=1, source_target_pairs={{0,16},{4,20},{8,24},{12,28},{16,0},{20,4},{24,8},{28,12},{1,17},{... | collective-permute-start | bytes 405512 | tf_op jit(solution)/shard_map/ppermute | solution.py:705
  61.9 5.5 %collective-permute-done.6.top_ref = bf16[528,128]{1,0:T(8,128)(2,1)S(1)} collective-permute-done((bf16[528,128]{1,0:T(8,128)(2,1)S(1)}, bf16[528,128]{1,0:T(8,128)(2,1)S(1)}, u32[]{:S(2)}, u32[]{:S(2)}) %collective-permute-start.6) | collective-permute-done | bytes 135200 | tf_op jit(solution)/shard_map/ppermute | solution.py:705
  67.8 1.6 %collective-permute-start.7 = (bf16[4,128,128]{2,1,0:T(8,128)(2,1)S(1)}, bf16[4,128,128]{2,1,0:T(8,128)(2,1)S(1)}, u32[]{:S(2)}, u32[]{:S(2)}) collective-permute-start(bf16[4,128,128]{2,1,0:T(8,128)(2,1)S(1)} %get-tuple-element.153), channel_id=1, source_target_pairs={{0,4},{4,0},{8,12},{12,8},{16,20},{20,16},{24,28},{28,24},{1,5},{5... | collective-permute-start | bytes 393224 | tf_op jit(solution)/shard_map/ppermute | solution.py:705
  69.5 3.6 %shard_map.252 = (f32[4,128,128]{2,1,0:T(8,128)S(1)}, f32[4,128,128]{2,1,0:T(8,128)S(1)}, f32[4,128,128]{2,1,0:T(8,128)S(1)}, f32[4,128,128]{2,1,0:T(8,128)S(1)}...) custom-call(s32[1]{0:T(128)} %bitcast.base_ref.here_ref._, ...), custom_call_target="tpu_custom_call" | custom-call | tf_op jit(solution)/shard_map/pallas_call | solution.py:684
  73.1 1.8 %shard_map.256 = (bf16[4,128,128]{2,1,0:T(8,128)(2,1)S(1)}, f32[4,128,128]{2,1,0:T(8,128)S(1)}, bf16[4,128,128]{2,1,0:T(8,128)(2,1)S(1)}, f32[128,128]{1,0:T(8,1...) custom-call(s32[1]{0:T(128)} %bitcast.base_ref.here_ref._, ...), custom_call_target="tpu_custom_call" | custom-call | tf_op jit(solution)/shard_map/pallas_call | solution.py:684
  74.9 2.1 %shard_map.257 = (bf16[4,128,128]{2,1,0:T(8,128)(2,1)S(1)}, f32[4,128,128]{2,1,0:T(8,128)S(1)}, bf16[4,128,128]{2,1,0:T(8,128)(2,1)S(1)}, f32[8,128]{1,0:T(8,128...) custom-call(s32[1]{0:T(128)} %bitcast.base_ref.here_ref._, ...), custom_call_target="tpu_custom_call", output_to_operand_aliasing={{6}: (18, {})} | custom-call | tf_op jit(solution)/shard_map/pallas_call | solution.py:684
  78.8 2.9 %collective-permute-done.9 = f32[2,128]{1,0:T(2,128)S(1)} collective-permute-done((f32[2,128]{1,0:T(2,128)S(1)}, f32[2,128]{1,0:T(2,128)S(1)}, u32[]{:S(2)}, u32[]{:S(2)}) %collective-permute-start.9) | collective-permute-done | bytes 1056 | tf_op jit(solution)/shard_map/ppermute | solution.py:705
  83.3 3.6 %collective-permute-done.17.moved_ref = bf16[2,128,512]{2,1,0:T(8,128)(2,1)S(1)} collective-permute-done((bf16[2,128,512]{2,1,0:T(8,128)(2,1)S(1)}, bf16[2,128,512]{2,1,0:T(8,128)(2,1)S(1)}, u32[]{:S(2)}, u32[]{:S(2)}) %collective-permute-start.17) | collective-permute-done | bytes 262176 | tf_op jit(solution)/shard_map/ppermute | solution.py:705
  87.0 1.6 %collective-permute-start.18 = (bf16[1,128,512]{2,1,0:T(8,128)(2,1)S(1)}, bf16[1,128,512]{2,1,0:T(8,128)(2,1)S(1)}, u32[]{:S(2)}, u32[]{:S(2)}) collective-permute-start(bf16[1,128,512]{2,1,0:T(8,128)(2,1)S(1)} %get-tuple-element.194), channel_id=1, source_target_pairs={{0,16},{4,20},{8,24},{12,28},{16,0},{20,4},{24,8},{28,12},{1,17},{... | collective-permute-start | bytes 393224 | tf_op jit(solution)/shard_map/ppermute | solution.py:705
  91.6 3.7 %collective-permute-done.11.moved_ref = f32[2,128]{1,0:T(2,128)S(1)} collective-permute-done((f32[2,128]{1,0:T(2,128)S(1)}, f32[2,128]{1,0:T(2,128)S(1)}, u32[]{:S(2)}, u32[]{:S(2)}) %collective-permute-start.11) | collective-permute-done | bytes 1056 | tf_op jit(solution)/shard_map/ppermute | solution.py:705
  (65 shorter events, 20.4 us)
Async XLA Ops:
  1.5 11.7 %collective-permute-start.13 = (bf16[1,128,512]{2,1,0:T(8,128)(2,1)S(1)}, bf16[1,128,512]{2,1,0:T(8,128)(2,1)S(1)}, u32[]{:S(2)}, u32[]{:S(2)}) collective-permute-start(bf16[1,128,512]{2,1,0:T(8,128)(2,1)S(1)} %shard_map.260.first_ref), channel_id=1, source_target_pairs={{0,16},{4,20},{8,24},{12,28},{16,0},{20,4},{24,8},{28,12},{1,17},{... | collective-permute-start | bytes 393224 | tf_op jit(solution)/shard_map/ppermute | solution.py:705
  5.7 30.7 %copy-start.5 = (bf16[1,128,1024]{2,1,0:T(8,128)(2,1)S(1)}, bf16[1,128,1024]{2,1,0:T(8,128)(2,1)}, u32[]{:S(2)}) copy-start(bf16[1,128,1024]{2,1,0:T(8,128)(2,1)} %param.14) | copy-start | bytes 786436
  11.7 7.8 %collective-permute-start = (bf16[4,128,256]{2,1,0:T(8,128)(2,1)S(1)}, bf16[4,128,256]{2,1,0:T(8,128)(2,1)S(1)}, u32[]{:S(2)}, u32[]{:S(2)}) collective-permute-start(bf16[4,128,256]{2,1,0:T(8,128)(2,1)S(1)} %get-tuple-element.107), channel_id=1, source_target_pairs={{0,4},{4,0},{8,12},{12,8},{16,20},{20,16},{24,28},{28,24},{1,5},{5... | collective-permute-start | bytes 786440 | tf_op jit(solution)/shard_map/ppermute | solution.py:705
  13.3 23.7 %copy-start.3 = (bf16[1,128,1024]{2,1,0:T(8,128)(2,1)S(1)}, bf16[1,128,1024]{2,1,0:T(8,128)(2,1)}, u32[]{:S(2)}) copy-start(bf16[1,128,1024]{2,1,0:T(8,128)(2,1)} %param.16) | copy-start | bytes 786436
  13.3 23.7 %copy-start.6 = (bf16[1,128,1024]{2,1,0:T(8,128)(2,1)S(1)}, bf16[1,128,1024]{2,1,0:T(8,128)(2,1)}, u32[]{:S(2)}) copy-start(bf16[1,128,1024]{2,1,0:T(8,128)(2,1)} %param.21) | copy-start | bytes 786436
  13.3 23.7 %copy-start.7 = (bf16[1,128,1024]{2,1,0:T(8,128)(2,1)S(1)}, bf16[1,128,1024]{2,1,0:T(8,128)(2,1)}, u32[]{:S(2)}) copy-start(bf16[1,128,1024]{2,1,0:T(8,128)(2,1)} %param.22) | copy-start | bytes 786436
  13.4 23.7 %copy-start.10 = (f32[128]{0:T(128)S(1)}, f32[128]{0:T(128)}, u32[]{:S(2)}) copy-start(f32[128]{0:T(128)} %param.20) | copy-start | bytes 1540
  13.4 8.1 %collective-permute-start.14 = (bf16[2,128,512]{2,1,0:T(8,128)(2,1)S(1)}, bf16[2,128,512]{2,1,0:T(8,128)(2,1)S(1)}, u32[]{:S(2)}, u32[]{:S(2)}) collective-permute-start(bf16[2,128,512]{2,1,0:T(8,128)(2,1)S(1)} %shard_map.261.first_ref), channel_id=1, source_target_pairs={{0,8},{4,12},{8,0},{12,4},{16,24},{20,28},{24,16},{28,20},{1,9},{5... | collective-permute-start | bytes 786440 | tf_op jit(solution)/shard_map/ppermute | solution.py:705
  19.9 7.0 %collective-permute-start.1 = (bf16[4,128,256]{2,1,0:T(8,128)(2,1)S(1)}, bf16[4,128,256]{2,1,0:T(8,128)(2,1)S(1)}, u32[]{:S(2)}, u32[]{:S(2)}) collective-permute-start(bf16[4,128,256]{2,1,0:T(8,128)(2,1)S(1)} %get-tuple-element.108.own_ref), channel_id=1, source_target_pairs={{0,8},{4,12},{8,0},{12,4},{16,24},{20,28},{24,16},{28,20},{1,9},{5... | collective-permute-start | bytes 786440 | tf_op jit(solution)/shard_map/ppermute | solution.py:705
  21.5 22.0 %collective-permute-start.15 = (bf16[4,128,512]{2,1,0:T(8,128)(2,1)S(1)}, bf16[4,128,512]{2,1,0:T(8,128)(2,1)S(1)}, u32[]{:S(2)}, u32[]{:S(2)}) collective-permute-start(bf16[4,128,512]{2,1,0:T(8,128)(2,1)S(1)} %shard_map.262.near_ref), channel_id=1, source_target_pairs={{0,4},{4,0},{8,12},{12,8},{16,20},{20,16},{24,28},{28,24},{1,5},{5... | collective-permute-start | bytes 1572872 | tf_op jit(solution)/shard_map/ppermute | solution.py:705
  27.1 7.3 %collective-permute-start.2 = (bf16[4,128,128]{2,1,0:T(8,128)(2,1)S(1)}, bf16[4,128,128]{2,1,0:T(8,128)(2,1)S(1)}, u32[]{:S(2)}, u32[]{:S(2)}) collective-permute-start(bf16[4,128,128]{2,1,0:T(8,128)(2,1)S(1)} %get-tuple-element.109), channel_id=1, source_target_pairs={{0,16},{4,20},{8,24},{12,28},{16,0},{20,4},{24,8},{28,12},{1,17},{... | collective-permute-start | bytes 393224 | tf_op jit(solution)/shard_map/ppermute | solution.py:705
  34.8 5.0 %collective-permute-start.3 = (bf16[4,128,128]{2,1,0:T(8,128)(2,1)S(1)}, bf16[4,128,128]{2,1,0:T(8,128)(2,1)S(1)}, u32[]{:S(2)}, u32[]{:S(2)}) collective-permute-start(bf16[4,128,128]{2,1,0:T(8,128)(2,1)S(1)} %get-tuple-element.112), channel_id=1, source_target_pairs={{0,4},{4,0},{8,12},{12,8},{16,20},{20,16},{24,28},{28,24},{1,5},{5... | collective-permute-start | bytes 393224 | tf_op jit(solution)/shard_map/ppermute | solution.py:705
  42.0 12.4 %collective-permute-start.4 = (bf16[528,128]{1,0:T(8,128)(2,1)S(1)}, bf16[528,128]{1,0:T(8,128)(2,1)S(1)}, u32[]{:S(2)}, u32[]{:S(2)}) collective-permute-start(bf16[528,128]{1,0:T(8,128)(2,1)S(1)} %get-tuple-element.137.mine_ref), channel_id=1, source_target_pairs={{0,4},{4,0},{8,12},{12,8},{16,20},{20,16},{24,28},{28,24},{1,5},{5... | collective-permute-start | bytes 405512 | tf_op jit(solution)/shard_map/ppermute | solution.py:705
  53.9 24.7 %collective-permute-start.16 = (bf16[4,128,512]{2,1,0:T(8,128)(2,1)S(1)}, bf16[4,128,512]{2,1,0:T(8,128)(2,1)S(1)}, u32[]{:S(2)}, u32[]{:S(2)}) collective-permute-start(bf16[4,128,512]{2,1,0:T(8,128)(2,1)S(1)} %get-tuple-element.190), channel_id=1, source_target_pairs={{0,4},{4,0},{8,12},{12,8},{16,20},{20,16},{24,28},{28,24},{1,5},{5... | collective-permute-start | bytes 1572872 | tf_op jit(solution)/shard_map/ppermute | solution.py:705
  54.7 5.1 %collective-permute-start.5 = (bf16[528,128]{1,0:T(8,128)(2,1)S(1)}, bf16[528,128]{1,0:T(8,128)(2,1)S(1)}, u32[]{:S(2)}, u32[]{:S(2)}) collective-permute-start(bf16[528,128]{1,0:T(8,128)(2,1)S(1)} %get-tuple-element.138.own_ref.mine_ref), channel_id=1, source_target_pairs={{0,8},{4,12},{8,0},{12,4},{16,24},{20,28},{24,16},{28,20},{1,9},{5... | collective-permute-start | bytes 405512 | tf_op jit(solution)/shard_map/ppermute | solution.py:705
  60.0 7.4 %collective-permute-start.6 = (bf16[528,128]{1,0:T(8,128)(2,1)S(1)}, bf16[528,128]{1,0:T(8,128)(2,1)S(1)}, u32[]{:S(2)}, u32[]{:S(2)}) collective-permute-start(bf16[528,128]{1,0:T(8,128)(2,1)S(1)} %get-tuple-element.139.mine_ref), channel_id=1, source_target_pairs={{0,16},{4,20},{8,24},{12,28},{16,0},{20,4},{24,8},{28,12},{1,17},{... | collective-permute-start | bytes 405512 | tf_op jit(solution)/shard_map/ppermute | solution.py:705
  67.8 7.0 %collective-permute-start.7 = (bf16[4,128,128]{2,1,0:T(8,128)(2,1)S(1)}, bf16[4,128,128]{2,1,0:T(8,128)(2,1)S(1)}, u32[]{:S(2)}, u32[]{:S(2)}) collective-permute-start(bf16[4,128,128]{2,1,0:T(8,128)(2,1)S(1)} %get-tuple-element.153), channel_id=1, source_target_pairs={{0,4},{4,0},{8,12},{12,8},{16,20},{20,16},{24,28},{28,24},{1,5},{5... | collective-permute-start | bytes 393224 | tf_op jit(solution)/shard_map/ppermute | solution.py:705
  77.0 1.2 %collective-permute-start.8 = (f32[2,128]{1,0:T(2,128)S(1)}, f32[2,128]{1,0:T(2,128)S(1)}, u32[]{:S(2)}, u32[]{:S(2)}) collective-permute-start(f32[2,128]{1,0:T(2,128)S(1)} %get-tuple-element.169), channel_id=1, source_target_pairs={{0,1},{1,0},{2,3},{3,2},{4,5},{5,4},{6,7},{7,6},{8,9},{9,8},{10,11... | collective-permute-start | bytes 3080 | tf_op jit(solution)/shard_map/ppermute | solution.py:705
  78.2 3.6 %collective-permute-start.9 = (f32[2,128]{1,0:T(2,128)S(1)}, f32[2,128]{1,0:T(2,128)S(1)}, u32[]{:S(2)}, u32[]{:S(2)}) collective-permute-start(f32[2,128]{1,0:T(2,128)S(1)} %add.9), channel_id=1, source_target_pairs={{0,4},{4,0},{8,12},{12,8},{16,20},{20,16},{24,28},{28,24},{1,5},{5... | collective-permute-start | bytes 3080 | tf_op jit(solution)/shard_map/ppermute | solution.py:705
  78.7 8.2 %collective-permute-start.17 = (bf16[2,128,512]{2,1,0:T(8,128)(2,1)S(1)}, bf16[2,128,512]{2,1,0:T(8,128)(2,1)S(1)}, u32[]{:S(2)}, u32[]{:S(2)}) collective-permute-start(bf16[2,128,512]{2,1,0:T(8,128)(2,1)S(1)} %get-tuple-element.192), channel_id=1, source_target_pairs={{0,8},{4,12},{8,0},{12,4},{16,24},{20,28},{24,16},{28,20},{1,9},{5... | collective-permute-start | bytes 786440 | tf_op jit(solution)/shard_map/ppermute | solution.py:705
  81.8 6.8 %collective-permute-start.10 = (f32[2,128]{1,0:T(2,128)S(1)}, f32[2,128]{1,0:T(2,128)S(1)}, u32[]{:S(2)}, u32[]{:S(2)}) collective-permute-start(f32[2,128]{1,0:T(2,128)S(1)} %select_add_fusion.1), channel_id=1, source_target_pairs={{0,8},{4,12},{8,0},{12,4},{16,24},{20,28},{24,16},{28,20},{1,9},{5... | collective-permute-start | bytes 3080 | tf_op jit(solution)/shard_map/ppermute | solution.py:705
  81.9 9.6 %collective-permute-start.12 = (f32[2,128]{1,0:T(2,128)S(1)}, f32[2,128]{1,0:T(2,128)S(1)}, u32[]{:S(2)}, u32[]{:S(2)}) collective-permute-start(f32[2,128]{1,0:T(2,128)S(1)} %add.9), channel_id=1, source_target_pairs={{0,2},{2,0},{1,3},{3,1},{4,6},{6,4},{5,7},{7,5},{8,10},{10,8},{9,1... | collective-permute-start | bytes 3080 | tf_op jit(solution)/shard_map/ppermute | solution.py:705
  87.0 8.8 %collective-permute-start.18 = (bf16[1,128,512]{2,1,0:T(8,128)(2,1)S(1)}, bf16[1,128,512]{2,1,0:T(8,128)(2,1)S(1)}, u32[]{:S(2)}, u32[]{:S(2)}) collective-permute-start(bf16[1,128,512]{2,1,0:T(8,128)(2,1)S(1)} %get-tuple-element.194), channel_id=1, source_target_pairs={{0,16},{4,20},{8,24},{12,28},{16,0},{20,4},{24,8},{28,12},{1,17},{... | collective-permute-start | bytes 393224 | tf_op jit(solution)/shard_map/ppermute | solution.py:705
  88.7 6.6 %collective-permute-start.11 = (f32[2,128]{1,0:T(2,128)S(1)}, f32[2,128]{1,0:T(2,128)S(1)}, u32[]{:S(2)}, u32[]{:S(2)}) collective-permute-start(f32[2,128]{1,0:T(2,128)S(1)} %select_add_fusion.sums_ref), channel_id=1, source_target_pairs={{0,16},{4,20},{8,24},{12,28},{16,0},{20,4},{24,8},{28,12},{1,17},{... | collective-permute-start | bytes 3080 | tf_op jit(solution)/shard_map/ppermute | solution.py:705
  (6 other events, 28.3 us)
